TPU v7x, 256 devices: a whole 4x4x8 slice. The times are simulated.
256 devices in a mesh: ctx: 16 (over y, x_lo, core), rep: 8 (over z), head: 2 (over x_hi).
Axes of the slice: x: 4 (x_hi: 2, x_lo: 2; x = x_hi * 2 + x_lo), y: 4, z: 8, core: 2. Of those that a mesh axis runs over, the one named last changes fastest.
Arguments:
- inputs: bfloat16 [8, 8192, 2048], P('rep', 'ctx', 'head'), may hold values from -6 to 6
- queries: bfloat16 [8, 8192, 2048], P('rep', 'ctx', 'head'), may hold values from -6 to 6
- keys: bfloat16 [8, 8192, 2048], P('rep', 'ctx', 'head'), may hold values from -6 to 6
- targets: bfloat16 [8, 8192, 2048], P('rep', 'ctx', 'head'), may hold values from -3 to 3
- value_weight: bfloat16 [8, 2048, 2048], P('rep', None, 'head'), may hold values from -0.125 to 0.125
- anchor: float32 [2048, 2048], P('ctx', 'head'), may hold values from -0.125 to 0.125
- momentum: float32 [2048, 2048], P('ctx', 'head'), may hold values from -6 to 6
Outputs:
- anchor_next: float32 [8, 2048, 2048], P('rep', 'ctx', 'head')
- momentum_next: float32 [8, 2048, 2048], P('rep', 'ctx', 'head')
All inputs are finite; a program needn't handle non-finite values.
Results may differ from a plain program's by a relative error of at most 0.02.
Values may be sent and summed in bfloat16 or wider, within the bound.
A program may use at most 64 MiB of HBM per device.

v0:
```python
import math

import jax
import jax.numpy as jnp
from jax import lax
from jax.sharding import PartitionSpec as P

HEAD_DIM = 128


inner_rate = 0.05
slow_decay = 0.5
outer_rate = 1.0


def carried_in(shard, axis, join, neutral, backward):
    count = lax.axis_size(axis)
    place = lax.axis_index(axis)
    ahead = count - 1 - place if backward else place
    gathered = lax.all_gather(shard.astype(jnp.bfloat16), axis)
    state = jnp.zeros_like(shard) + jnp.asarray(neutral, shard.dtype)

    def one(turn, state):
        source = count - 1 - turn if backward else turn
        return join(state, lax.dynamic_index_in_dim(gathered, source, 0, False).astype(shard.dtype))

    return lax.fori_loop(0, ahead, one, state)


def from_partner(block, axis, apart):
    count = lax.axis_size(axis)
    route = []
    for low in range(count):
        high = low | 1 << apart
        if high != low and high < count:
            route += [(low, high), (high, low)]
    return lax.ppermute(block, axis, route)


def add_states(earlier, later):
    return earlier + later


def carried(local_state, forward):
    empty = jnp.zeros_like(local_state)
    if forward:
        return carried_in(local_state, "ctx", add_states, empty, False)
    return carried_in(local_state, "ctx", add_states, empty, True)


def mix_total(delta):
    for bit_number in range(2):
        delta = (
            delta + from_partner(delta.astype(jnp.bfloat16), "rep", bit_number).astype(delta.dtype)
        ) * 0.5
    return delta


def mix_rows(delta):
    return mix_total(delta)


def local(inputs, queries, keys, targets, value_weight, anchor, momentum):
    n_blocks = lax.axis_size("ctx")
    tokens_here = queries.shape[1]
    local_width = queries.shape[2]
    heads_here = local_width // HEAD_DIM
    sequence = tokens_here * n_blocks
    attn_scale = 1.0 / math.sqrt(HEAD_DIM * sequence)
    loss_scale = 1.0 / math.sqrt(sequence)
    weights_local = value_weight[0]
    model_width = weights_local.shape[0]
    share_rows = model_width // n_blocks
    first_row = lax.axis_index("ctx") * share_rows
    weight_rows = lax.dynamic_slice_in_dim(weights_local, first_row, share_rows, 0).astype(
        jnp.float32
    )
    drift = (anchor - weight_rows) / inner_rate
    features = lax.all_gather(inputs, "head", axis=2, tiled=True)[0]
    values = jnp.dot(features, weights_local, preferred_element_type=jnp.float32).astype(
        jnp.bfloat16
    )
    query_heads = queries[0].reshape(tokens_here, heads_here, HEAD_DIM)
    key_heads = keys[0].reshape(tokens_here, heads_here, HEAD_DIM)
    value_heads = values.reshape(tokens_here, heads_here, HEAD_DIM)
    target_heads = targets[0].reshape(tokens_here, heads_here, HEAD_DIM)
    scores = jnp.einsum("thd,shd->hts", query_heads, key_heads, preferred_element_type=jnp.float32)
    causal = jnp.arange(tokens_here)[:, None] >= jnp.arange(tokens_here)[None, :]
    weighted = jnp.where(causal[None], scores, 0.0).astype(jnp.bfloat16)
    local_state = jnp.einsum(
        "shd,she->hde", key_heads, value_heads, preferred_element_type=jnp.float32
    )
    prefix_state = carried(local_state, True)
    outputs = attn_scale * (
        jnp.einsum("hts,she->the", weighted, value_heads, preferred_element_type=jnp.float32)
        + jnp.einsum(
            "thd,hde->the",
            query_heads,
            prefix_state.astype(jnp.bfloat16),
            preferred_element_type=jnp.float32,
        )
    )
    grad_out = (loss_scale * (outputs - target_heads.astype(jnp.float32))).astype(jnp.bfloat16)
    back_local = jnp.einsum(
        "thd,the->hde", query_heads, grad_out, preferred_element_type=jnp.float32
    )
    suffix_state = carried(back_local, False)
    grad_values = attn_scale * (
        jnp.einsum("hts,the->she", weighted, grad_out, preferred_element_type=jnp.float32)
        + jnp.einsum(
            "shd,hde->she",
            key_heads,
            suffix_state.astype(jnp.bfloat16),
            preferred_element_type=jnp.float32,
        )
    )
    grad_values = grad_values.astype(jnp.bfloat16).reshape(tokens_here, local_width)
    gradient = lax.psum_scatter(
        lax.dot_general(
            features, grad_values, (((0,), (0,)), ((), ())), preferred_element_type=jnp.float32
        ).astype(jnp.bfloat16),
        "ctx",
        scatter_dimension=0,
        tiled=True,
    ).astype(jnp.float32)
    mixed = mix_rows(drift + gradient)
    momentum_next = slow_decay * momentum + mixed
    anchor_next = anchor - outer_rate * inner_rate * momentum_next
    return (anchor_next[None], momentum_next[None])


def solution(mesh):
    placed = (
        P("rep", "ctx", "head"),
        P("rep", "ctx", "head"),
        P("rep", "ctx", "head"),
        P("rep", "ctx", "head"),
        P("rep", None, "head"),
        P("ctx", "head"),
        P("ctx", "head"),
    )
    return jax.shard_map(
        local,
        mesh=mesh,
        in_specs=placed,
        out_specs=(P("rep", "ctx", "head"), P("rep", "ctx", "head")),
        check_vma=False,
    )
```

profile of v0, /device:TPU:4, one launch (start us, length us, event | category | flops | bytes accessed | tf_op | source)
XLA Modules:
  0.0 287.8 jit_solution(1893113426766698581)
XLA Ops:
  7.9 1.5 copy.54
  9.4 40.3 %all-gather.6.cloned.1.call-done = bf16[1,512,2048]{2,1,0:T(8,128)(2,1)} async-done(((bf16[1,512,1024]{2,1,0:T(8,128)(2,1)}), bf16[1,512,2048]{2,1,0:T(8,128)(2,1)}) %all-gather.6.cloned.1.call-update) | async-done | bytes 2097168 | tf_op jit(solution)/shard_map/all_gather | solution.py:79
  49.8 5.2 %fusion.6 = bf16[512,1024]{1,0:T(8,128)(2,1)S(1)} fusion(bf16[1,2048,1024]{2,1,0:T(8,128)(2,1)} %param.15, bf16[1,512,2048]{2,1,0:T(8,128)(2,1)} %all-gather.6.cloned.1.call-done), kind=kOutput, calls=%fused_computation.12 | convolution fusion | flops 2148007936 | bytes 7340032 | tf_op jit(solution)/shard_map/dot_general | solution.py:80
  56.9 1.5 copy.53
  58.4 3.0 %copy.38 = f32[1,512,1024]{1,2,0:T(8,128)} copy(bf16[1,512,1024]{2,1,0:T(8,128)(2,1)} %param.14) | data formatting | bytes 3145728 | tf_op jit(solution)/shard_map/convert_element_type | solution.py:103
  61.5 1.4 select_convert_fusion
  62.8 1.9 copy-done
  64.8 1.5 fusion.25
  66.3 32.3 %all-gather.8.cloned.1.call-done = bf16[128,128,128]{2,1,0:T(8,128)(2,1)} async-done(((bf16[8,128,128]{2,1,0:T(8,128)(2,1)}), bf16[128,128,128]{2,1,0:T(8,128)(2,1)}) %all-gather.8.cloned.1.call-update) | async-done | bytes 4194320 | tf_op jit(solution)/shard_map/all_gather | solution.py:20
  98.6 2.6 fusion.3
  103.7 3.2 %fusion.26 = f32[8,128,512]{2,1,0:T(8,128)S(1)} fusion(bf16[512,8,128]{0,2,1:T(8,128)(2,1)} %copy-done.1, bf16[8,512,512]{2,1,0:T(8,128)(2,1)} %copy-done), kind=kOutput, calls=%fused_computation.37 | convolution fusion | flops 536870912 | bytes 7340032 | tf_op jit(solution)/shard_map/hts,the->she/dot_general | solution.py:109
  106.9 52.1 %all-gather.10.cloned.1.call-done = bf16[128,128,128]{2,1,0:T(8,128)(2,1)} async-done(((bf16[8,128,128]{2,1,0:T(8,128)(2,1)}), bf16[128,128,128]{2,1,0:T(8,128)(2,1)}) %all-gather.10.cloned.1.call-update) | async-done | bytes 4194320 | tf_op jit(solution)/shard_map/all_gather | solution.py:20
  159.0 16.5 %while.23 = (s32[]{:T(128)}, f32[8,128,128]{2,1,0:T(8,128)S(1)}, s32[]{:T(128)}, bf16[16,8,128,128]{3,2,1,0:T(8,128)(2,1)}, s32[]{:T(128)}, /*index=5*/s32[]{:T(128)}, s32[]{:T(128)}, s32[]{:T(128)}) while((s32[]{:T(128)}, f32[8,128,128]{2,1,0:T(8,128)S(1)}, s32[]{:T(128)}, bf16[16,8,128,128]{3,2,1,0:T(8,128)(2,1)}, s32[]{:T(128)}, ...), condition=%wide.region_3.4_spmd, body=%wide.region_2.3_spmd.sunk | while | flops 262150 | bytes 1310855 | solution.py:27
  159.1 1.1 convert_add_fusion.5
  160.2 1.1 convert_add_fusion.5
  161.3 1.1 convert_add_fusion.5
  165.6 1.1 convert_add_fusion.5
  166.7 1.1 convert_add_fusion.5
  167.8 1.1 convert_add_fusion.5
  168.9 1.1 convert_add_fusion.5
  170.0 1.1 convert_add_fusion.5
  171.1 1.1 convert_add_fusion.5
  172.2 1.1 convert_add_fusion.5
  175.5 1.9 multiply_convert_fusion
  177.4 4.3 %convert_bitcast_fusion = bf16[2048,1024]{0,1:T(8,128)(2,1)} fusion(bf16[512,1024]{0,1:T(8,128)(2,1)S(1)} %bitcast.81, bf16[1,512,2048]{2,1,0:T(8,128)(2,1)S(1)} %copy-done.7), kind=kOutput, calls=%fused_computation.5 | convolution fusion | flops 2149580800 | bytes 7340032 | tf_op jit(solution)/shard_map/dot_general | solution.py:119
  181.8 6.4 %copy.49 = bf16[2048,1024]{1,0:T(8,128)(2,1)} copy(bf16[2048,1024]{0,1:T(8,128)(2,1)} %convert_bitcast_fusion) | data formatting | bytes 8388608
  189.6 70.3 %reduce-scatter.4.cloned.1.call-done = bf16[128,1024]{1,0:T(8,128)(2,1)} async-done(((bf16[2048,1024]{1,0:T(8,128)(2,1)}), bf16[128,1024]{1,0:T(8,128)(2,1)}) %reduce-scatter.4.cloned.1.call-update) | async-done | bytes 262160
  259.9 1.1 copy.50
  261.2 1.7 collective-permute-start
  262.9 4.8 %collective-permute-done = bf16[128,1024]{0,1:T(8,128)(2,1)S(1)} collective-permute-done((bf16[128,1024]{0,1:T(8,128)(2,1)S(1)}, bf16[128,1024]{0,1:T(8,128)(2,1)S(1)}, u32[]{:S(2)}, u32[]{:S(2)}) %collective-permute-start) | collective-permute-done | bytes 262176 | tf_op jit(solution)/shard_map/ppermute | solution.py:37
  267.8 3.4 %collective-permute-start.1 = (bf16[128,1024]{0,1:T(8,128)(2,1)S(1)}, bf16[128,1024]{0,1:T(8,128)(2,1)S(1)}, u32[]{:S(2)}, u32[]{:S(2)}) collective-permute-start(bf16[128,1024]{0,1:T(8,128)(2,1)S(1)} %fusion.21), channel_id=1, source_target_pairs={{0,4},{4,0},{2,6},{6,2},{8,12},{12,8},{10,14},{14,10},{1,5},{5,1},... | collective-permute-start | bytes 786440 | tf_op jit(solution)/shard_map/ppermute | solution.py:37
  271.4 7.6 %collective-permute-done.1 = bf16[128,1024]{0,1:T(8,128)(2,1)S(1)} collective-permute-done((bf16[128,1024]{0,1:T(8,128)(2,1)S(1)}, bf16[128,1024]{0,1:T(8,128)(2,1)S(1)}, u32[]{:S(2)}, u32[]{:S(2)}) %collective-permute-start.1) | collective-permute-done | bytes 262176 | tf_op jit(solution)/shard_map/ppermute | solution.py:37
  (46 shorter events, 14.6 us)
Async XLA Ops:
  7.2 42.6 %all-gather.6.cloned.1.call-start = ((), (), s32[]{:S(2)}) async-start(), calls=%async_computation.1 | async-start | bytes 3145728 | tf_op jit(solution)/shard_map/all_gather | solution.py:79
  7.9 90.7 %all-gather.8.cloned.1.call-start = ((), (), s32[]{:S(2)}) async-start(), calls=%async_computation.2 | async-start | bytes 4456448 | tf_op jit(solution)/shard_map/all_gather | solution.py:20
  9.4 52.0 %copy-start.2 = (bf16[64,8,8,128]{3,2,1,0:T(8,128)(2,1)}, bf16[64,8,8,128]{3,2,1,0:T(8,128)(2,1)S(1)}, u32[]{:S(2)}) copy-start(bf16[64,8,8,128]{3,2,1,0:T(8,128)(2,1)S(1)} %copy.54) | copy-start | bytes 3145732
  56.8 102.2 %all-gather.10.cloned.1.call-start = ((), (), s32[]{:S(2)}) async-start(), calls=%async_computation.3 | async-start | bytes 4456448 | tf_op jit(solution)/shard_map/all_gather | solution.py:20
  58.4 3.1 %copy-start.3 = (bf16[64,8,8,128]{3,2,1,0:T(8,128)(2,1)}, bf16[64,8,8,128]{3,2,1,0:T(8,128)(2,1)S(1)}, u32[]{:S(2)}) copy-start(bf16[64,8,8,128]{3,2,1,0:T(8,128)(2,1)S(1)} %copy.53) | copy-start | bytes 3145732
  62.8 1.9 copy-start
  98.6 3.6 %copy-start.4 = (bf16[64,8,8,128]{3,2,1,0:T(8,128)(2,1)S(1)}, bf16[64,8,8,128]{3,2,1,0:T(8,128)(2,1)}, u32[]{:S(2)}) copy-start(bf16[64,8,8,128]{3,2,1,0:T(8,128)(2,1)} %copy-done.3) | copy-start | bytes 3145732
  101.3 1.0 copy-start.1
  103.6 156.3 %reduce-scatter.4.cloned.1.call-start = ((), (), s32[]{:S(2)}) async-start(), calls=%async_computation.4 | async-start | bytes 4456448
  175.5 1.9 copy-start.7
  188.2 1.2 copy-start.5
  189.4 81.8 %copy-start.6 = (f32[128,1024]{1,0:T(8,128)S(1)}, f32[128,1024]{1,0:T(8,128)}, u32[]{:S(2)}) copy-start(f32[128,1024]{1,0:T(8,128)} %param.17) | copy-start | bytes 1572868
  261.2 6.5 %collective-permute-start = (bf16[128,1024]{0,1:T(8,128)(2,1)S(1)}, bf16[128,1024]{0,1:T(8,128)(2,1)S(1)}, u32[]{:S(2)}, u32[]{:S(2)}) collective-permute-start(bf16[128,1024]{0,1:T(8,128)(2,1)S(1)} %fusion.24), channel_id=1, source_target_pairs={{0,2},{2,0},{4,6},{6,4},{8,10},{10,8},{12,14},{14,12},{1,3},{3,1},... | collective-permute-start | bytes 786440 | tf_op jit(solution)/shard_map/ppermute | solution.py:37
  267.8 11.2 %collective-permute-start.1 = (bf16[128,1024]{0,1:T(8,128)(2,1)S(1)}, bf16[128,1024]{0,1:T(8,128)(2,1)S(1)}, u32[]{:S(2)}, u32[]{:S(2)}) collective-permute-start(bf16[128,1024]{0,1:T(8,128)(2,1)S(1)} %fusion.21), channel_id=1, source_target_pairs={{0,4},{4,0},{2,6},{6,2},{8,12},{12,8},{10,14},{14,10},{1,5},{5,1},... | collective-permute-start | bytes 786440 | tf_op jit(solution)/shard_map/ppermute | solution.py:37
Sparse Core Ops, SparseCore 0:
  9.8 39.9 all-gather.5
  56.9 41.5 all-gather.7
  103.7 55.2 all-gather.9
  188.3 71.5 reduce-scatter.3
where the time goes:
time: 290 us; the launch traced here: 288 us
  waiting for transfers between devices  208 us (72%)
  local copies, waits for them, and re-layouts  22.3 us (8%)
  matrix products  21 us (7%)
  other arithmetic  16.6 us (6%)
  between operations  14 us (5%)
  starting transfers between devices  5.24 us (2%)
    all_gather x2, waiting for transfers between devices, carried_in(): gathered = lax.all_gather(shard.astype(jnp.bfloat16), axis)  84.4 us
    unnamed x5, waiting for transfers between devices  71 us
    all_gather x1, waiting for transfers between devices, local(): features = lax.all_gather(inputs, 'head', axis=2, tiled=True)[0]  40.3 us
    add x15, other arithmetic, add_states(): return earlier + later  16 us
    unnamed x25, local copies, waits for them, and re-layouts  16 us
    ppermute x2, waiting for transfers between devices, from_partner(): return lax.ppermute(block, axis, route)  12.4 us
  transfers between devices with their start and end apart: 6, of which 6 were waited for; matrix products, arithmetic and copies ran while one was open for 5% of the time, Pallas kernels for 0%

commit v1 on v0

v1 whole, which is shorter than its diff:
```python
import functools
import math

import jax
import jax.numpy as jnp
from jax import lax
from jax.experimental import pallas as pl
from jax.experimental.pallas import tpu as pltpu
from jax.sharding import PartitionSpec as P

HEAD_DIM = 128
GROUPS = 4
CHUNKS = 4
MESH = pl.DeviceIdType.MESH

inner_rate = 0.05
slow_decay = 0.5
outer_rate = 1.0

F32 = jnp.float32
BF16 = jnp.bfloat16


def dot(a, b):
    return jnp.dot(a, b, preferred_element_type=F32)


def lanes(index, size=HEAD_DIM):
    return pl.ds(pl.multiple_of(index * size, size), size)


def kernel(
    attn_scale,
    loss_scale,
    x_ref,
    q_ref,
    k_ref,
    t_ref,
    w_ref,
    a_ref,
    out_ref,
    x2,
    xp,
    xt,
    rel,
    qv,
    kv,
    tv,
    wv,
    av,
    qt,
    kt,
    sc,
    sct,
    wqk,
    vp,
    vv,
    gl,
    base,
    st,
    cr,
    tt,
    yr,
    xs,
    xr,
    ps,
    pr,
    gv,
    s1,
    r1,
    s2,
    r2,
    own,
    sx,
    rx,
    dz,
    rz,
    mz,
    mixb,
    load_sem,
    f_send,
    f_recv,
    p_send,
    p_recv,
    c_send,
    c_recv,
    y_send,
    y_recv,
    x_send,
    x_recv,
    b_send,
    b_recv,
    g_send,
    g_recv,
    r1_send,
    r1_recv,
    r2_send,
    r2_recv,
    rx_send,
    rx_recv,
    rz_send,
    rz_recv,
    mz_send,
    mz_recv,
):
    tokens, width = qv.shape
    half = x2.shape[2]
    heads = width // HEAD_DIM
    per_group = heads // GROUPS
    mine = per_group // 2
    cols = per_group * HEAD_DIM
    rows_dev = av.shape[0]
    gc = loss_scale * attn_scale

    me = lax.axis_index("ctx")
    rep = lax.axis_index("rep")
    head = lax.axis_index("head")
    core = lax.rem(me, 2)
    xl = lax.rem(me // 2, 2)
    y = me // 4
    low = lax.rem(me, 4)
    core_peer = (me + 1 - 2 * core, rep, head)
    x_id = me + 2 - 4 * xl
    x_peer = (x_id, rep, head)
    far_peer = (x_id, rep, 1 - head)
    y_up = (lax.rem(y + 1, 4) * 4 + low, rep, head)
    y_down = (lax.rem(y + 3, 4) * 4 + low, rep, head)
    zk = lax.rem(rep, 4)
    z_ids = [lax.rem(zk + d, 4) for d in (1, 2, 3)]
    z_peers = [(me, rep - zk + z, head) for z in z_ids]

    def remote(src, dst, send, recv, peer):
        return pltpu.make_async_remote_copy(
            src_ref=src, dst_ref=dst, send_sem=send, recv_sem=recv, device_id=peer, device_id_type=MESH
        )

    own_rows = pl.ds(pl.multiple_of(head * half, half), half)
    other_rows = pl.ds(pl.multiple_of((1 - head) * half, half), half)
    loads = [
        pltpu.make_async_copy(src, dst, load_sem.at[n])
        for n, (src, dst) in enumerate(
            (
                (q_ref, qv),
                (k_ref, kv),
                (x_ref, x2.at[0]),
                (w_ref.at[own_rows], wv.at[0]),
                (t_ref, tv),
                (w_ref.at[other_rows], wv.at[1]),
                (w_ref.at[pl.ds(pl.multiple_of(me * rows_dev, rows_dev), rows_dev)], wv.at[2, pl.ds(0, rows_dev)]),
                (a_ref, av),
            )
        )
    ]
    for copy in loads:
        copy.start()

    yr[...] = jnp.zeros_like(yr)

    barrier = pltpu.get_barrier_semaphore()
    peers = [core_peer, x_peer, far_peer, y_up, y_down, *z_peers]
    for peer in peers:
        pl.semaphore_signal(barrier, inc=1, device_id=peer, device_id_type=MESH)

    pl.semaphore_wait(barrier, len(peers))

    piece = tokens // 2 // CHUNKS
    first = []
    for n in range(CHUNKS):
        for side, peer in ((0, x_peer), (1, far_peer)):
            at = side * (tokens // 2) + n * piece
            first.append(
                remote(x_ref.at[pl.ds(at, piece)], rel.at[side, n], f_send.at[side, n], f_recv.at[side, n], peer)
            )
            first[-1].start()
    swaps = []
    for n in range(4):
        src = x_ref.at[:, lanes(2 * n + 1 - core)]
        swaps.append(remote(src, xp.at[head * 4 + n], p_send.at[0, n], p_recv.at[0, n], core_peer))
        swaps[-1].start()

    second = []

    def relay(n):
        for side, peer in ((0, far_peer), (1, x_peer)):
            first[2 * n + side].wait_recv()
            at = side * (tokens // 2) + n * piece
            second.append(
                remote(
                    rel.at[side, n],
                    x2.at[1, pl.ds(at, piece)],
                    f_send.at[2 + side, n],
                    f_recv.at[2 + side, n],
                    peer,
                )
            )
            second[-1].start()

    loads[0].wait()
    loads[1].wait()
    mid = tokens // 2

    def scores(h, carry):
        at = lanes(h)
        q = qv[:, at]
        k = kv[:, at]
        q_t = q.T
        k_t = k.T
        qt[h] = q_t
        kt[h] = k_t
        row = lax.broadcasted_iota(jnp.int32, (mid, mid), 0)
        col = lax.broadcasted_iota(jnp.int32, (mid, mid), 1)
        lower = row >= col
        upper = row <= col
        for n in range(2):
            rows = slice(n * mid, (n + 1) * mid)
            sc[h, rows, rows] = jnp.where(lower, dot(q[rows], k_t[:, rows]), 0.0).astype(BF16)
            sct[h, rows, rows] = jnp.where(upper, dot(k[rows], q_t[:, rows]), 0.0).astype(BF16)
        sc[h, mid:, :mid] = dot(q[mid:], k_t[:, :mid]).astype(BF16)
        sct[h, :mid, mid:] = dot(k[:mid], q_t[:, mid:]).astype(BF16)
        wqk[h, :mid, :HEAD_DIM] = (gc * dot(sct[h, :mid, :], q)).astype(BF16)
        wqk[h, mid:, :HEAD_DIM] = (gc * dot(sct[h, mid:, mid:], q[mid:])).astype(BF16)
        wqk[h, :, HEAD_DIM:] = k
        st[0, h] = dot(q_t, q).astype(BF16)
        return carry

    lax.fori_loop(0, heads, scores, 0)

    pending = []

    def heads_of(g, which):
        return pl.ds(g * per_group + which * mine, mine)

    def scan_core(kind, g):
        copy = remote(
            st.at[kind, heads_of(g, 1 - core)], cr.at[kind, g], c_send.at[kind, g], c_recv.at[kind, g], core_peer
        )
        copy.start()
        pending.append(copy)

    def y_copy(kind, g, n, src, peer):
        return remote(src, yr.at[kind, n, g], y_send.at[kind, n, g], y_recv.at[kind, n, g], peer)

    def y_copies(kind, g):
        ahead, behind = (y_up, y_down) if kind == 1 else (y_down, y_up)
        return (
            y_copy(kind, g, 0, tt.at[kind, g], ahead),
            y_copy(kind, g, 1, yr.at[kind, 0, g], ahead),
            y_copy(kind, g, 2, tt.at[kind, g], behind),
        )

    def place(kind):
        return y if kind == 1 else 3 - y

    def scan_y(kind, g):
        remote(
            st.at[kind, heads_of(g, 1 - core)], cr.at[kind, g], c_send.at[kind, g], c_recv.at[kind, g], core_peer
        ).wait_recv()
        total = st[kind, heads_of(g, core)].astype(F32) + cr[kind, g].astype(F32)
        tt[kind, g] = total.astype(BF16)
        step, _, wrap = y_copies(kind, g)
        pl.when(place(kind) < 3)(step.start)
        pl.when(place(kind) == 0)(wrap.start)

    def scan_relay(kind, g):
        step, pass_on, _ = y_copies(kind, g)
        pl.when(place(kind) > 0)(step.wait_recv)
        pl.when((place(kind) == 1) | (place(kind) == 2))(pass_on.start)

    def x_copy(kind, g):
        return remote(xs.at[kind, g], xr.at[kind, g], x_send.at[kind, g], x_recv.at[kind, g], x_peer)

    def earlier(kind, g):
        return yr[kind, 0, g].astype(F32) + yr[kind, 1, g].astype(F32) + yr[kind, 2, g].astype(F32)

    def scan_x(kind, g):
        _, pass_on, wrap = y_copies(kind, g)
        pl.when(place(kind) > 1)(pass_on.wait_recv)
        pl.when(place(kind) == 3)(wrap.wait_recv)
        gives = (xl == 0) if kind == 1 else (xl == 1)
        sent = earlier(kind, g) + jnp.where(gives, tt[kind, g].astype(F32), 0.0)
        xs[kind, g] = sent.astype(BF16)
        copy = x_copy(kind, g)
        copy.start()
        pending.append(copy)

    def b_copy(kind, g):
        return remote(
            ps.at[kind, g], pr.at[kind, heads_of(g, core)], b_send.at[kind, g], b_recv.at[kind, g], core_peer
        )

    def scan_back(kind, g):
        x_copy(kind, g).wait_recv()
        chip = earlier(kind, g) + xr[kind, g].astype(F32)
        later = (core == 1) if kind == 1 else (core == 0)
        mine_too = st[kind, heads_of(g, core)].astype(F32)
        theirs = cr[kind, g].astype(F32)
        ps[kind, g] = jnp.where(later, chip, chip + mine_too).astype(BF16)
        pr[kind, heads_of(g, core)] = jnp.where(later, chip + theirs, chip).astype(BF16)
        copy = b_copy(kind, g)
        copy.start()
        pending.append(copy)

    def scan_end(kind, g):
        b_copy(kind, g).wait_recv()

    for g in range(GROUPS):
        scan_core(0, g)

    relay(0)
    relay(1)

    loads[2].wait()
    loads[3].wait()
    wide = 256

    def partial(n, carry):
        at = lanes(n, wide)
        vp[:, at] = dot(x2[0], wv[0, :, at])
        return carry

    lax.fori_loop(0, width // wide, partial, 0)

    for g in range(GROUPS):
        scan_y(0, g)
    relay(2)
    relay(3)

    def turn_own(side):
        def turn(n, carry):
            at = lanes(((head + side) % 2) * 4 + n)
            xt[at, :tokens] = x2[side, :, lanes(2 * n + core)].T
            return carry

        lax.fori_loop(0, 4, turn, 0)

    def turn_theirs(side):
        def turn(n, carry):
            block = ((head + side) % 2) * 4 + n
            xt[lanes(block), tokens:] = xp[block].T
            return carry

        lax.fori_loop(0, 4, turn, 0)

    turn_own(0)
    for g in range(GROUPS):
        scan_relay(0, g)
    for copy in swaps:
        copy.wait_recv()
    turn_theirs(0)
    loads[4].wait()
    loads[5].wait()
    for g in range(GROUPS):
        scan_x(0, g)

    def finish(n):
        for side in range(2):
            for m in (2 * n, 2 * n + 1):
                second[2 * m + side].wait_recv()
        size = 2 * piece

        def values(m, carry):
            at = lanes(m, wide)
            for side in range(2):
                rows = slice(side * mid + n * size, side * mid + (n + 1) * size)
                vv[rows, at] = (vp[rows, at] + dot(x2[1, rows, :], wv[1, :, at])).astype(BF16)
            return carry

        lax.fori_loop(0, width // wide, values, 0)

    finish(0)
    finish(1)
    for n in range(4):
        src = x2.at[1, :, lanes(2 * n + 1 - core)]
        swaps.append(remote(src, xp.at[(1 - head) * 4 + n], p_send.at[1, n], p_recv.at[1, n], core_peer))
        swaps[-1].start()
    for g in range(GROUPS):
        scan_back(0, g)
    for g in range(GROUPS):
        scan_end(0, g)

    def states(h, carry):
        at = lanes(h)
        v = vv[:, at]
        state = dot(kt[h], v).astype(BF16)
        st[1, h] = state
        top = dot(sc[h, :mid, :mid], v[:mid])
        bottom = dot(sc[h, mid:, :], v)
        scaled = loss_scale * attn_scale
        gl[:mid, at] = (scaled * top - loss_scale * tv[:mid, at].astype(F32)).astype(BF16)
        gl[mid:, at] = (scaled * bottom - loss_scale * tv[mid:, at].astype(F32)).astype(BF16)
        st[2, h] = (dot(qt[h], gl[:, at]) + gc * dot(pr[0, h], state)).astype(BF16)
        return carry

    def bases(h, carry):
        at = lanes(h)
        base[:mid, at] = dot(sct[h, :mid, :], gl[:, at])
        base[mid:, at] = dot(sct[h, mid:, mid:], gl[mid:, at])
        return carry

    def over(body, g):
        lax.fori_loop(g * per_group, (g + 1) * per_group, body, 0)

    def gv_copy(g):
        return remote(gv.at[g, pl.ds(0, tokens)], gv.at[g, pl.ds(tokens, tokens)], g_send.at[g], g_recv.at[g], core_peer)

    def grads(g):
        def one(n, carry):
            h = g * per_group + n
            at = lanes(h)
            prefix = pr[1, h]
            both = (prefix.astype(F32) + st[1, h].astype(F32)).astype(BF16)
            suffix = (gc * dot(pr[0, h], both) + pr[2, h].astype(F32)).astype(BF16)
            pair = jnp.concatenate([prefix, suffix], axis=0)
            gv[g, :tokens, lanes(n)] = (attn_scale * (base[:, at] + dot(wqk[h], pair))).astype(BF16)
            return carry

        lax.fori_loop(0, per_group, one, 0)
        copy = gv_copy(g)
        copy.start()
        pending.append(copy)

    two = 2 * rows_dev
    part = cols // 2

    def block(g, to):
        return dot(xt[pl.ds(pl.multiple_of(to * two, two), two), :], gv[g])

    def r1_copies(g):
        return (
            remote(s1.at[g, 0], r1.at[g, 0], r1_send.at[g, 0], r1_recv.at[g, 0], y_up),
            remote(s1.at[g, 1], r1.at[g, 1], r1_send.at[g, 1], r1_recv.at[g, 1], y_down),
        )

    def r2_copies(g):
        return (
            remote(s2.at[g, 0], r2.at[g, 0], r2_send.at[g, 0], r2_recv.at[g, 0], y_up),
            remote(s2.at[g, 1], r2.at[g, 1], r2_send.at[g, 1], r2_recv.at[g, 1], y_down),
        )

    def reduce_one(g):
        gv_copy(g).wait_recv()
        across = block(g, lax.rem(y + 2, 4)).astype(BF16)
        s1[g, 0] = across[:, :part]
        s1[g, 1] = across[:, part:]
        for copy in r1_copies(g):
            copy.start()
            pending.append(copy)

    def reduce_two(g):
        up = block(g, lax.rem(y + 1, 4))
        down = block(g, lax.rem(y + 3, 4))
        one = r1_copies(g)
        s2[g, 0, :, part:] = up[:, part:].astype(BF16)
        s2[g, 1, :, :part] = down[:, :part].astype(BF16)
        one[0].wait_recv()
        s2[g, 0, :, :part] = (up[:, :part] + r1[g, 0].astype(F32)).astype(BF16)
        one[1].wait_recv()
        s2[g, 1, :, part:] = (down[:, part:] + r1[g, 1].astype(F32)).astype(BF16)
        for copy in r2_copies(g):
            copy.start()
            pending.append(copy)
        own[g] = block(g, y)

    def rx_copy(g):
        return remote(sx.at[g], rx.at[g], rx_send.at[g], rx_recv.at[g], x_peer)

    def block_rows(which):
        return pl.ds(pl.multiple_of(which * rows_dev, rows_dev), rows_dev)

    def reduce_x(g):
        for copy in r2_copies(g):
            copy.wait_recv()
        rows = block_rows(1 - xl)
        sx[g] = (own[g, rows, :] + r2[g, 0, rows, :].astype(F32) + r2[g, 1, rows, :].astype(F32)).astype(BF16)
        copy = rx_copy(g)
        copy.start()
        pending.append(copy)

    share = rows_dev // 4

    def piece_rows(which):
        return pl.ds(pl.multiple_of(which * share, share), share)

    def rz_copies(g):
        return [
            remote(dz.at[g, piece_rows(z)], rz.at[g, n], rz_send.at[g, n], rz_recv.at[g, n], peer)
            for n, (z, peer) in enumerate(zip(z_ids, z_peers))
        ]

    def reduce_z(g):
        rx_copy(g).wait_recv()
        rows = block_rows(xl)
        at = slice(g * cols, (g + 1) * cols)
        total = own[g, rows, :] + r2[g, 0, rows, :].astype(F32) + r2[g, 1, rows, :].astype(F32)
        drift = (av[:, at] - wv[2, :rows_dev, at].astype(F32)) / inner_rate
        dz[g] = (total + rx[g].astype(F32) + drift).astype(BF16)
        for copy in rz_copies(g):
            copy.start()
            pending.append(copy)

    def mz_copies(g):
        at = slice(g * cols, (g + 1) * cols)
        return [
            remote(mz.at[g], mixb.at[piece_rows(zk), at], mz_send.at[g, n], mz_recv.at[g, n], peer)
            for n, peer in enumerate(z_peers)
        ]

    def mix(g):
        for copy in rz_copies(g):
            copy.wait_recv()
        at = slice(g * cols, (g + 1) * cols)
        total = dz[g, piece_rows(zk), :].astype(F32)
        for n in range(3):
            total += rz[g, n].astype(F32)
        mean = (0.25 * total).astype(BF16)
        mz[g] = mean
        mixb[piece_rows(zk), at] = mean
        for copy in mz_copies(g):
            copy.start()
            pending.append(copy)

    def settle(g):
        for copy in mz_copies(g):
            copy.wait_recv()

    kinds = (1, 2)

    def each(stage):
        def run(g):
            for kind in kinds:
                stage(kind, g)

        return run

    loads[6].wait()
    loads[7].wait()

    def start_group(g):
        over(states, g)
        for kind in kinds:
            scan_core(kind, g)

    def prepare():
        turn_own(1)
        for copy in swaps[4:]:
            copy.wait_recv()
        turn_theirs(1)

    def end_group(g):
        for kind in kinds:
            scan_end(kind, g)
        grads(g)

    stages = [
        start_group,
        each(scan_y),
        each(scan_relay),
        each(scan_x),
        each(scan_back),
        end_group,
        reduce_one,
        reduce_two,
        reduce_x,
        reduce_z,
        mix,
        settle,
    ]
    for turn in range(GROUPS + len(stages) - 1):
        for n in range(len(stages) - 1, -1, -1):
            g = turn - n
            if 0 <= g < GROUPS:
                stages[n](g)
        if turn < GROUPS:
            over(bases, turn)
        if turn == GROUPS - 1:
            prepare()

    out_ref[...] = mixb[...].astype(F32)

    for copy in first + second + swaps + pending:
        copy.wait_send()
    for kind in range(3):
        for g in range(GROUPS):
            step, pass_on, wrap = y_copies(kind, g)
            pl.when(place(kind) < 3)(step.wait_send)
            pl.when((place(kind) == 1) | (place(kind) == 2))(pass_on.wait_send)
            pl.when(place(kind) == 0)(wrap.wait_send)


def mixed_delta(x, q, k, t, w, a, attn_scale, loss_scale):
    tokens, half = x.shape
    width = q.shape[1]
    heads = width // HEAD_DIM
    rows_dev = a.shape[0]
    groups = GROUPS
    per_group = heads // groups
    mine = per_group // 2
    cols = per_group * HEAD_DIM
    two = 2 * rows_dev
    piece = tokens // 2 // CHUNKS
    state = (HEAD_DIM, HEAD_DIM)
    vmem = pltpu.VMEM
    dma = pltpu.SemaphoreType.DMA
    scratch = [
        vmem((2, tokens, half), BF16),
        vmem((8, tokens, HEAD_DIM), BF16),
        vmem((8 * HEAD_DIM, 2 * tokens), BF16),
        vmem((2, CHUNKS, piece, half), BF16),
        vmem((tokens, width), BF16),
        vmem((tokens, width), BF16),
        vmem((tokens, width), BF16),
        vmem((3, half, width), BF16),
        vmem((rows_dev, width), F32),
        vmem((heads, HEAD_DIM, tokens), BF16),
        vmem((heads, HEAD_DIM, tokens), BF16),
        vmem((heads, tokens, tokens), BF16),
        vmem((heads, tokens, tokens), BF16),
        vmem((heads, tokens, 2 * HEAD_DIM), BF16),
        vmem((tokens, width), F32),
        vmem((tokens, width), BF16),
        vmem((tokens, width), BF16),
        vmem((tokens, width), F32),
        vmem((3, heads, *state), BF16),
        vmem((3, groups, mine, *state), BF16),
        vmem((3, groups, mine, *state), BF16),
        vmem((3, 3, groups, mine, *state), BF16),
        vmem((3, groups, mine, *state), BF16),
        vmem((3, groups, mine, *state), BF16),
        vmem((3, groups, mine, *state), BF16),
        vmem((3, heads, *state), BF16),
        vmem((groups, 2 * tokens, cols), BF16),
        vmem((groups, 2, two, cols // 2), BF16),
        vmem((groups, 2, two, cols // 2), BF16),
        vmem((groups, 2, two, cols), BF16),
        vmem((groups, 2, two, cols), BF16),
        vmem((groups, two, cols), F32),
        vmem((groups, rows_dev, cols), BF16),
        vmem((groups, rows_dev, cols), BF16),
        vmem((groups, rows_dev, cols), BF16),
        vmem((groups, 3, rows_dev // 4, cols), BF16),
        vmem((groups, rows_dev // 4, cols), BF16),
        vmem((rows_dev, width), BF16),
        dma((8,)),
        dma((4, CHUNKS)),
        dma((4, CHUNKS)),
        dma((2, 4)),
        dma((2, 4)),
        dma((3, groups)),
        dma((3, groups)),
        dma((3, 3, groups)),
        dma((3, 3, groups)),
        dma((3, groups)),
        dma((3, groups)),
        dma((3, groups)),
        dma((3, groups)),
        dma((groups,)),
        dma((groups,)),
        dma((groups, 2)),
        dma((groups, 2)),
        dma((groups, 2)),
        dma((groups, 2)),
        dma((groups,)),
        dma((groups,)),
        dma((groups, 3)),
        dma((groups, 3)),
        dma((groups, 3)),
        dma((groups, 3)),
    ]
    return pl.pallas_call(
        functools.partial(kernel, attn_scale, loss_scale),
        out_shape=jax.ShapeDtypeStruct((rows_dev, width), F32),
        in_specs=[pl.BlockSpec(memory_space=pl.ANY)] * 6,
        out_specs=pl.BlockSpec(memory_space=pltpu.VMEM),
        scratch_shapes=scratch,
        compiler_params=pltpu.CompilerParams(
            collective_id=0, has_side_effects=True, vmem_limit_bytes=60 * 1024 * 1024
        ),
    )(x, q, k, t, w, a)


def local(inputs, queries, keys, targets, value_weight, anchor, momentum):
    sequence = queries.shape[1] * lax.axis_size("ctx")
    attn_scale = 1.0 / math.sqrt(HEAD_DIM * sequence)
    loss_scale = 1.0 / math.sqrt(sequence)
    mixed = mixed_delta(
        inputs[0], queries[0], keys[0], targets[0], value_weight[0], anchor, attn_scale, loss_scale
    )
    momentum_next = slow_decay * momentum + mixed
    anchor_next = anchor - outer_rate * inner_rate * momentum_next
    return (anchor_next[None], momentum_next[None])


def solution(mesh):
    placed = (
        P("rep", "ctx", "head"),
        P("rep", "ctx", "head"),
        P("rep", "ctx", "head"),
        P("rep", "ctx", "head"),
        P("rep", None, "head"),
        P("ctx", "head"),
        P("ctx", "head"),
    )
    return jax.shard_map(
        local,
        mesh=mesh,
        in_specs=placed,
        out_specs=(P("rep", "ctx", "head"), P("rep", "ctx", "head")),
        check_vma=False,
    )
```

time: 290 us -> 93.8 us (0.32)
  waiting for transfers between devices: 208 us -> 0 us
  Pallas kernels: 0 us -> 90.9 us
  local copies, waits for them, and re-layouts: 22.3 us -> 0.01 us
  matrix products: 21 us -> 0 us
  other arithmetic: 16.6 us -> 2.18 us
  between operations: 14 us -> 0.67 us
  starting transfers between devices: 5.24 us -> 0 us
    all_gather x3 -> x0, waiting for transfers between devices: 125 us -> none  [the longest x2 84.4 us: carried_in(): gathered = lax.all_gather(shard.astype(jnp.bfloat16), axis)]
    pallas_call x0 -> x1, Pallas kernels: none -> 90.9 us  [mixed_delta(): pl.pallas_call(functools.partial(kernel, attn_scale, loss_scale), out_sha...]
    unnamed x5 -> x0, waiting for transfers between devices: 71 us -> none
    dot_general x9 -> x0, matrix products: 21 us -> none  [the longest x1 5.15 us: local(): jnp.dot(features, weights_local, preferred_element_type=jnp.float32)]
    add x15 -> x0, other arithmetic: 16 us -> none  [add_states(): return earlier + later]
    unnamed x25 -> x4, local copies, waits for them, and re-layouts: 16 us -> 0.01 us
    ppermute x2 -> x0, waiting for transfers between devices: 12.4 us -> none  [from_partner(): return lax.ppermute(block, axis, route)]
    ppermute x2 -> x0, starting transfers between devices: 5.08 us -> none  [from_partner(): return lax.ppermute(block, axis, route)]
  transfers between devices with their start and end apart: 6 -> 0, of which waited for: 6 -> 0; matrix products, arithmetic and copies ran while one was open for 5% -> 0% of each run, Pallas kernels for 0% -> 0%
where the time goes in v1:
time: 93.8 us; the launch traced here: 93.7 us
  Pallas kernels  90.9 us (97%)
  other arithmetic  2.18 us (2%)
    pallas_call x1, Pallas kernels, mixed_delta(): pl.pallas_call(functools.partial(kernel, attn_scale, loss_scale), out_sha...  90.9 us
    broadcast_in_dim x1, other arithmetic, local(): return (anchor_next[None], momentum_next[None])  2.18 us

profile of v1, /device:TPU:4, one launch (start us, length us, event | category | flops | bytes accessed | tf_op | source)
XLA Modules:
  0.0 93.7 jit_solution(13897403511923123253)
XLA Ops:
  0.6 0.0 copy-start
  0.6 0.0 copy-start.1
  0.7 90.9 %shard_map.86 = f32[128,1024]{1,0:T(8,128)} custom-call(bf16[512,1024]{1,0:T(8,128)(2,1)} %bitcast.10, bf16[512,1024]{1,0:T(8,128)(2,1)} %bitcast.11, bf16[512,1024]{1,0:T(8,128)(2,1)} %bitcast.12, bf16[512,1024]{1,0:T(8,128)(2,1)} %bitcast.13, bf16[2048,1024]{1,0:T(8,128)(2,1)} %bitcast.9, f32[128,1024]{1,0:T(8,128)} %a_ref.1), custom_call_target="tpu_custom_call" | custom-call | tf_op jit(solution)/shard_map/pallas_call | solution.py:669
  91.5 0.0 copy-done
  91.5 0.0 copy-done.1
  91.5 2.2 %fusion = (f32[1,128,1024]{2,1,0:T(8,128)}, f32[1,128,1024]{2,1,0:T(8,128)}) fusion(f32[128,1024]{1,0:T(8,128)} %shard_map.86, f32[128,1024]{1,0:T(8,128)S(1)} %copy-done.1, f32[128,1024]{1,0:T(8,128)S(1)} %copy-done), kind=kLoop, calls=%fused_computation.2 | loop fusion | flops 524288 | bytes 2621440 | tf_op jit(solution)/shard_map/broadcast_in_dim | solution.py:690
Async XLA Ops:
  0.6 90.9 %copy-start = (f32[128,1024]{1,0:T(8,128)S(1)}, f32[128,1024]{1,0:T(8,128)}, u32[]{:S(2)}) copy-start(f32[128,1024]{1,0:T(8,128)} %a_ref.1) | copy-start | bytes 1572868
  0.6 90.9 %copy-start.1 = (f32[128,1024]{1,0:T(8,128)S(1)}, f32[128,1024]{1,0:T(8,128)}, u32[]{:S(2)}) copy-start(f32[128,1024]{1,0:T(8,128)} %param.13) | copy-start | bytes 1572868

commit v2 on v1

v2 whole, which is shorter than its diff:
```python
import functools
import math

import jax
import jax.numpy as jnp
from jax import lax
from jax.experimental import pallas as pl
from jax.experimental.pallas import tpu as pltpu
from jax.sharding import PartitionSpec as P

HEAD_DIM = 128
GROUPS = 4
CHUNKS = 4
MESH = pl.DeviceIdType.MESH

ORDER = (
    ("state", 0), ("later", 0), ("state", 1), ("a_rest", 0), ("y", 0), ("state", 2), ("later", 1), ("state", 3),
    ("later", 2), ("y", 1), ("later", 3), ("x", 0), ("base", 0), ("y", 2), ("base", 1), ("y", 3), ("x", 1),
    ("back", 0), ("prepare", 0), ("x", 2), ("know", 0), ("grad", 0), ("x", 3), ("back", 1), ("r1", 0), ("base", 2), ("sides", 0),
    ("grad", 1), ("back", 2), ("r1", 1), ("r2", 0), ("back", 3), ("base", 3), ("grad", 2), ("own", 0), ("sides", 1), ("r1", 2),
    ("r2", 1), ("grad", 3), ("rx", 0), ("r1", 3), ("sides", 2), ("r2", 2), ("own", 1), ("sides", 3), ("know_all", 0), ("rz", 0), ("r2", 3),
    ("rx", 1), ("own", 2), ("rz", 1), ("own", 3), ("rx", 2), ("mix", 0), ("rz", 2), ("mix", 1), ("rx", 3), ("rz", 3), ("end", 0), ("mix", 2), ("end", 1),
    ("mix", 3), ("end", 2), ("end", 3),
)

inner_rate = 0.05
slow_decay = 0.5
outer_rate = 1.0

F32 = jnp.float32
BF16 = jnp.bfloat16


def dot(a, b):
    return jnp.dot(a, b, preferred_element_type=F32)


def lanes(index, size=HEAD_DIM):
    return pl.ds(pl.multiple_of(index * size, size), size)


def kernel(
    attn_scale,
    loss_scale,
    x_ref,
    q_ref,
    k_ref,
    t_ref,
    w_ref,
    a_ref,
    out_ref,
    x2,
    xp,
    xt,
    rel,
    qv,
    kv,
    tv,
    wv,
    av,
    qt,
    kt,
    sc,
    sct,
    wqk,
    vp,
    vv,
    gl,
    base,
    st,
    cr,
    tt,
    yr,
    xs,
    xr,
    ps,
    pr,
    gv,
    keep,
    s1,
    r1,
    s2,
    r2,
    own,
    sx,
    rx,
    dz,
    rz,
    mz,
    mixb,
    uu,
    load_sem,
    sent,
    f_recv,
    p_recv,
    a_recv,
    ay_recv,
    c_recv,
    y_recv,
    x_recv,
    b_recv,
    g_recv,
    r1_recv,
    r2_recv,
    rx_recv,
    rz_recv,
    mz_recv,
    y_known,
    low_known,
    high_known,
):
    tokens, width = qv.shape
    half = x2.shape[2]
    heads = width // HEAD_DIM
    per_group = heads // GROUPS
    mine = per_group // 2
    cols = per_group * HEAD_DIM
    rows_dev = av.shape[0]
    gc = loss_scale * attn_scale

    me = lax.axis_index("ctx")
    rep = lax.axis_index("rep")
    head = lax.axis_index("head")
    core = lax.rem(me, 2)
    xl = lax.rem(me // 2, 2)
    y = me // 4
    low = lax.rem(me, 4)
    core_peer = (me + 1 - 2 * core, rep, head)
    x_id = me + 2 - 4 * xl
    x_peer = (x_id, rep, head)
    far_peer = (x_id, rep, 1 - head)
    y_up = (lax.rem(y + 1, 4) * 4 + low, rep, head)
    y_down = (lax.rem(y + 3, 4) * 4 + low, rep, head)
    zk = lax.rem(rep, 4)
    y_far = (lax.rem(y + 2, 4) * 4 + low, rep, head)
    z_up = (me, lax.rem(rep + 1, 8), head)
    z_down = (me, lax.rem(rep + 7, 8), head)
    z_ids = [lax.rem(zk + d, 4) for d in (1, 2, 3)]
    z_peers = [(me, rep - zk + z, head) for z in z_ids]

    def remote(src, dst, send, recv, peer):
        return pltpu.make_async_remote_copy(
            src_ref=src, dst_ref=dst, send_sem=send, recv_sem=recv, device_id=peer, device_id_type=MESH
        )

    own_rows = pl.ds(pl.multiple_of(head * half, half), half)
    other_rows = pl.ds(pl.multiple_of((1 - head) * half, half), half)
    loads = [
        pltpu.make_async_copy(src, dst, load_sem.at[n])
        for n, (src, dst) in enumerate(
            (
                (q_ref, qv),
                (k_ref, kv),
                (x_ref, x2.at[0]),
                (w_ref.at[own_rows], wv.at[0]),
                (t_ref, tv),
                (w_ref.at[other_rows], wv.at[1]),
                (w_ref.at[pl.ds(pl.multiple_of(me * rows_dev, rows_dev), rows_dev)], wv.at[2, pl.ds(0, rows_dev)]),
                (a_ref, av),
            )
        )
    ]
    for copy in loads:
        copy.start()

    yr[...] = jnp.zeros_like(yr)

    barrier = pltpu.get_barrier_semaphore()
    peers = [core_peer, x_peer, far_peer, y_up, y_down, z_up, z_down]
    for peer in peers:
        pl.semaphore_signal(barrier, inc=1, device_id=peer, device_id_type=MESH)

    pl.semaphore_wait(barrier, len(peers))

    def tell(sem, peer):
        pl.semaphore_signal(sem, inc=1, device_id=peer, device_id_type=MESH)

    piece = tokens // 2 // CHUNKS
    first = []
    for n in range(CHUNKS):
        for side, peer in ((0, x_peer), (1, far_peer)):
            at = side * (tokens // 2) + n * piece
            first.append(
                remote(x_ref.at[pl.ds(at, piece)], rel.at[side, n], sent.at[0], f_recv.at[side, n], peer)
            )
            first[-1].start()
    swaps = []
    for n in range(4):
        src = x_ref.at[:, lanes(2 * n + 1 - core)]
        swaps.append(remote(src, xp.at[head * 4 + n], sent.at[2], p_recv.at[0, n], core_peer))
        swaps[-1].start()

    tell(y_known, y_down)
    inner = (zk > 0) & (zk < 3)

    @pl.when(inner)
    def _():
        tell(low_known, z_down)
        tell(high_known, z_up)

    second = []

    def relay(n):
        for side, peer in ((0, far_peer), (1, x_peer)):
            first[2 * n + side].wait_recv()
            at = side * (tokens // 2) + n * piece
            second.append(
                remote(
                    rel.at[side, n],
                    x2.at[1, pl.ds(at, piece)],
                    sent.at[1],
                    f_recv.at[2 + side, n],
                    peer,
                )
            )
            second[-1].start()

    loads[0].wait()
    loads[1].wait()
    mid = tokens // 2

    def scores(h, carry):
        at = lanes(h)
        q = qv[:, at]
        k = kv[:, at]
        q_t = q.T
        k_t = k.T
        qt[h] = q_t
        kt[h] = k_t
        row = lax.broadcasted_iota(jnp.int32, (mid, mid), 0)
        col = lax.broadcasted_iota(jnp.int32, (mid, mid), 1)
        lower = row >= col
        upper = row <= col
        for n in range(2):
            rows = slice(n * mid, (n + 1) * mid)
            sc[h, rows, rows] = jnp.where(lower, dot(q[rows], k_t[:, rows]), 0.0).astype(BF16)
            sct[h, rows, rows] = jnp.where(upper, dot(k[rows], q_t[:, rows]), 0.0).astype(BF16)
        sc[h, mid:, :mid] = dot(q[mid:], k_t[:, :mid]).astype(BF16)
        sct[h, :mid, mid:] = dot(k[:mid], q_t[:, mid:]).astype(BF16)
        wqk[h, :mid, :HEAD_DIM] = (gc * dot(sct[h, :mid, :], q)).astype(BF16)
        wqk[h, mid:, :HEAD_DIM] = (gc * dot(sct[h, mid:, mid:], q[mid:])).astype(BF16)
        wqk[h, :, HEAD_DIM:] = k
        st[0, h // per_group, lax.rem(h, per_group) // mine, lax.rem(h, mine)] = dot(q_t, q).astype(BF16)
        return carry

    lax.fori_loop(0, heads, scores, 0)

    both = pl.ds(1, 2)
    alone = pl.ds(0, 1)

    def place(kind):
        return y if kind == 1 else 3 - y

    def core_copy(kinds, g, sem, recv):
        return remote(st.at[kinds, g, 1 - core], cr.at[kinds, g], sent.at[sem], recv, core_peer)

    def y_copies(kind, g, recv, sem):
        ahead, behind = (y_up, y_down) if kind == 1 else (y_down, y_up)
        return [
            remote(tt.at[kind, g], yr.at[kind, d, g], sent.at[sem + d], recv.at[d], peer)
            for d, peer in enumerate((ahead, y_far, behind))
        ]

    def y_send(kind, g, recv, sem):
        total = st[kind, g, core].astype(F32) + cr[kind, g].astype(F32)
        tt[kind, g] = total.astype(BF16)
        for d, copy in enumerate(y_copies(kind, g, recv, sem)):
            pl.when(place(kind) < 3 - d)(copy.start)

    def y_wait(kind, g, recv, sem):
        for d, copy in enumerate(y_copies(kind, g, recv, sem)):
            pl.when(place(kind) > d)(copy.wait_recv)

    def earlier(kind, g):
        return yr[kind, 0, g].astype(F32) + yr[kind, 1, g].astype(F32) + yr[kind, 2, g].astype(F32)

    def x_fill(kind, g):
        gives = (xl == 0) if kind == 1 else (xl == 1)
        xs[kind, g] = (earlier(kind, g) + jnp.where(gives, tt[kind, g].astype(F32), 0.0)).astype(BF16)

    def x_copy(kinds, g, sem, recv):
        return remote(xs.at[kinds, g], xr.at[kinds, g], sent.at[sem], recv, x_peer)

    def back_fill(kind, g):
        chip = earlier(kind, g) + xr[kind, g].astype(F32)
        later = (core == 1) if kind == 1 else (core == 0)
        ours = st[kind, g, core].astype(F32)
        theirs = cr[kind, g].astype(F32)
        ps[kind, g] = jnp.where(later, chip, chip + ours).astype(BF16)
        pr[kind, g, core] = jnp.where(later, chip + theirs, chip).astype(BF16)

    def back_copy(kinds, g, sem, recv):
        return remote(ps.at[kinds, g], pr.at[kinds, g, core], sent.at[sem], recv, core_peer)

    every = pl.ds(0, GROUPS)
    head_start = pl.ds(0, 1)
    rest = pl.ds(1, GROUPS - 1)
    a_core = core_copy(alone, every, 3, a_recv.at[0])
    a_x = [x_copy(alone, part, 4, a_recv.at[1 + n]) for n, part in enumerate((head_start, rest))]
    a_back = [back_copy(alone, part, 5, a_recv.at[3 + n]) for n, part in enumerate((head_start, rest))]
    ay = (0, every, ay_recv, 6)
    a_core.start()

    relay(0)
    relay(1)

    loads[2].wait()
    loads[3].wait()
    wide = 256

    def partial(n, carry):
        at = lanes(n, wide)
        vp[:, at] = dot(x2[0], wv[0, :, at])
        return carry

    lax.fori_loop(0, width // wide, partial, 0)

    a_core.wait_recv()
    pl.semaphore_wait(y_known, 1)
    y_send(*ay)
    relay(2)
    relay(3)

    def turn_own(side):
        def turn(n, carry):
            at = lanes(((head + side) % 2) * 4 + n)
            xt[at, :tokens] = x2[side, :, lanes(2 * n + core)].T
            return carry

        lax.fori_loop(0, 4, turn, 0)

    def turn_theirs(side):
        def turn(n, carry):
            block = ((head + side) % 2) * 4 + n
            xt[lanes(block), tokens:] = xp[block].T
            return carry

        lax.fori_loop(0, 4, turn, 0)

    turn_own(0)
    for copy in swaps:
        copy.wait_recv()
    turn_theirs(0)
    loads[4].wait()
    loads[5].wait()
    y_wait(*ay)
    x_fill(0, head_start)
    a_x[0].start()
    x_fill(0, rest)

    def finish(n):
        for side in range(2):
            for m in (2 * n, 2 * n + 1):
                second[2 * m + side].wait_recv()
        if n == 1:
            a_x[1].start()
        size = 2 * piece

        def values(m, carry):
            at = lanes(m, wide)
            for side in range(2):
                rows = slice(side * mid + n * size, side * mid + (n + 1) * size)
                vv[rows, at] = (vp[rows, at] + dot(x2[1, rows, :], wv[1, :, at])).astype(BF16)
            return carry

        lax.fori_loop(0, width // wide, values, 0)

    finish(0)
    finish(1)
    for n in range(4):
        src = x2.at[1, :, lanes(2 * n + 1 - core)]
        swaps.append(remote(src, xp.at[(1 - head) * 4 + n], sent.at[2], p_recv.at[1, n], core_peer))
        swaps[-1].start()
    a_x[0].wait_recv()
    back_fill(0, head_start)
    a_back[0].start()

    def states(h, carry):
        at = lanes(h)
        g, which, n = h // per_group, lax.rem(h, per_group) // mine, lax.rem(h, mine)
        v = vv[:, at]
        st[1, g, which, n] = dot(kt[h], v).astype(BF16)
        top = dot(sc[h, :mid, :mid], v[:mid])
        bottom = dot(sc[h, mid:, :], v)
        gl[:mid, at] = (gc * top - loss_scale * tv[:mid, at].astype(F32)).astype(BF16)
        gl[mid:, at] = (gc * bottom - loss_scale * tv[mid:, at].astype(F32)).astype(BF16)
        uu[h] = dot(qt[h], gl[:, at])
        return carry

    def with_later(h, carry):
        g, which, n = h // per_group, lax.rem(h, per_group) // mine, lax.rem(h, mine)
        st[2, g, which, n] = (uu[h] + gc * dot(pr[0, g, which, n], st[1, g, which, n])).astype(BF16)
        return carry

    def bases(h, carry):
        at = lanes(h)
        base[:mid, at] = dot(sct[h, :mid, :], gl[:, at])
        base[mid:, at] = dot(sct[h, mid:, mid:], gl[mid:, at])
        return carry

    def over(body, g):
        lax.fori_loop(g * per_group, (g + 1) * per_group, body, 0)

    def gv_copy(g):
        return remote(
            gv.at[g, pl.ds(0, tokens)], gv.at[g, pl.ds(tokens, tokens)], sent.at[18], g_recv.at[g], core_peer
        )

    def grads(g):
        def one(n, carry):
            h = g * per_group + n
            at = lanes(h)
            which, i = n // mine, lax.rem(n, mine)
            prefix = pr[1, g, which, i]
            up_to = (prefix.astype(F32) + st[1, g, which, i].astype(F32)).astype(BF16)
            suffix = (gc * dot(pr[0, g, which, i], up_to) + pr[2, g, which, i].astype(F32)).astype(BF16)
            pair = jnp.concatenate([prefix, suffix], axis=0)
            gv[g, :tokens, lanes(n)] = (attn_scale * (base[:, at] + dot(wqk[h], pair))).astype(BF16)
            return carry

        lax.fori_loop(0, per_group, one, 0)
        copy = gv_copy(g)
        copy.start()

    two = 2 * rows_dev
    part = cols // 2

    def block(g, to):
        return dot(xt[pl.ds(pl.multiple_of(to * two, two), two), :], gv[g])

    def r1_copies(g):
        return (
            remote(s1.at[g, 0], r1.at[g, 0], sent.at[19], r1_recv.at[g, 0], y_up),
            remote(s1.at[g, 1], r1.at[g, 1], sent.at[19], r1_recv.at[g, 1], y_down),
        )

    def r2_copies(g):
        return (
            remote(s2.at[g, 0], r2.at[g, 0], sent.at[20], r2_recv.at[g, 0], y_up),
            remote(s2.at[g, 1], r2.at[g, 1], sent.at[20], r2_recv.at[g, 1], y_down),
        )

    def reduce_one(g):
        gv_copy(g).wait_recv()
        across = block(g, lax.rem(y + 2, 4)).astype(BF16)
        s1[g, 0] = across[:, :part]
        s1[g, 1] = across[:, part:]
        for copy in r1_copies(g):
            copy.start()

    def sides(g):
        up = block(g, lax.rem(y + 1, 4))
        s2[g, 0, :, part:] = up[:, part:].astype(BF16)
        keep[g, 0] = up[:, :part]
        down = block(g, lax.rem(y + 3, 4))
        s2[g, 1, :, :part] = down[:, :part].astype(BF16)
        keep[g, 1] = down[:, part:]

    def reduce_two(g):
        one = r1_copies(g)
        one[0].wait_recv()
        s2[g, 0, :, :part] = (keep[g, 0] + r1[g, 0].astype(F32)).astype(BF16)
        one[1].wait_recv()
        s2[g, 1, :, part:] = (keep[g, 1] + r1[g, 1].astype(F32)).astype(BF16)
        for copy in r2_copies(g):
            copy.start()

    def own_block(g):
        own[g] = block(g, y)

    def rx_copy(g):
        return remote(sx.at[g], rx.at[g], sent.at[21], rx_recv.at[g], x_peer)

    def block_rows(which):
        return pl.ds(pl.multiple_of(which * rows_dev, rows_dev), rows_dev)

    def reduce_x(g):
        for copy in r2_copies(g):
            copy.wait_recv()
        rows = block_rows(1 - xl)
        sx[g] = (own[g, rows, :] + r2[g, 0, rows, :].astype(F32) + r2[g, 1, rows, :].astype(F32)).astype(BF16)
        copy = rx_copy(g)
        copy.start()

    share = rows_dev // 4

    def piece_rows(which):
        return pl.ds(pl.multiple_of(which * share, share), share)

    def rz_copies(g):
        return [
            remote(dz.at[g, piece_rows(z)], rz.at[g, n], sent.at[22], rz_recv.at[g, n], peer)
            for n, (z, peer) in enumerate(zip(z_ids, z_peers))
        ]

    def reduce_z(g):
        rx_copy(g).wait_recv()
        rows = block_rows(xl)
        at = slice(g * cols, (g + 1) * cols)
        total = own[g, rows, :] + r2[g, 0, rows, :].astype(F32) + r2[g, 1, rows, :].astype(F32)
        drift = (av[:, at] - wv[2, :rows_dev, at].astype(F32)) / inner_rate
        dz[g] = (total + rx[g].astype(F32) + drift).astype(BF16)
        for copy in rz_copies(g):
            copy.start()

    def mz_copies(g):
        at = slice(g * cols, (g + 1) * cols)
        return [
            remote(mz.at[g], mixb.at[piece_rows(zk), at], sent.at[23], mz_recv.at[g, n], peer)
            for n, peer in enumerate(z_peers)
        ]

    def mix(g):
        for copy in rz_copies(g):
            copy.wait_recv()
        at = slice(g * cols, (g + 1) * cols)
        total = dz[g, piece_rows(zk), :].astype(F32)
        for n in range(3):
            total += rz[g, n].astype(F32)
        mean = (0.25 * total).astype(BF16)
        mz[g] = mean
        mixb[piece_rows(zk), at] = mean
        for copy in mz_copies(g):
            copy.start()

    def settle(g):
        for copy in mz_copies(g):
            copy.wait_recv()

    loads[6].wait()
    loads[7].wait()

    def scan_core(g):
        return core_copy(both, pl.ds(g, 1), 9, c_recv.at[g])

    def scan_x(g):
        return x_copy(both, pl.ds(g, 1), 10, x_recv.at[g])

    def scan_back(g):
        return back_copy(both, pl.ds(g, 1), 11, b_recv.at[g])

    def y_args(kind, g):
        return (kind, pl.ds(g, 1), y_recv.at[kind - 1, g], 12 + 3 * (kind - 1))

    def state_step(g):
        over(states, g)

    def later_step(g):
        if g < 2:
            a_back[g].wait_recv()
        over(with_later, g)
        scan_core(g).start()

    def later_states():
        a_x[1].wait_recv()
        back_fill(0, rest)
        a_back[1].start()

    def y_step(g):
        scan_core(g).wait_recv()
        for kind in (1, 2):
            y_send(*y_args(kind, g))

    def x_step(g):
        for kind in (1, 2):
            y_wait(*y_args(kind, g))
            x_fill(kind, pl.ds(g, 1))
        scan_x(g).start()

    def back_step(g):
        scan_x(g).wait_recv()
        for kind in (1, 2):
            back_fill(kind, pl.ds(g, 1))
        scan_back(g).start()

    def grad_step(g):
        scan_back(g).wait_recv()
        grads(g)

    def base_step(g):
        over(bases, g)

    def prepare(g):
        turn_own(1)
        for copy in swaps[4:]:
            copy.wait_recv()
        turn_theirs(1)

    def know(g):
        @pl.when(zk == 1)
        def _():
            pl.semaphore_wait(low_known, 1)
            tell(low_known, z_down)

        @pl.when(zk == 2)
        def _():
            pl.semaphore_wait(high_known, 1)
            tell(high_known, z_up)

    def know_all(g):
        @pl.when(zk == 0)
        def _():
            pl.semaphore_wait(low_known, 2)

        @pl.when(zk == 3)
        def _():
            pl.semaphore_wait(high_known, 2)

    steps = {
        "state": state_step,
        "later": later_step,
        "a_rest": lambda g: later_states(),
        "y": y_step,
        "x": x_step,
        "back": back_step,
        "base": base_step,
        "prepare": prepare,
        "know": know,
        "know_all": know_all,
        "grad": grad_step,
        "r1": reduce_one,
        "sides": sides,
        "r2": reduce_two,
        "own": own_block,
        "rx": reduce_x,
        "rz": reduce_z,
        "mix": mix,
        "end": settle,
    }
    for name, g in ORDER:
        steps[name](g)

    out_ref[...] = mixb[...]

    def drain(sem, ref):
        remote(ref, ref, sent.at[sem], sent.at[sem], core_peer).wait_send()

    drain(0, rel)
    drain(1, x2.at[1])
    drain(2, xp)
    drain(3, cr.at[alone])
    drain(4, xs.at[alone])
    drain(5, ps.at[alone])
    for kind in range(3):
        for d in range(3):
            sem = 6 + d if kind == 0 else 12 + 3 * (kind - 1) + d
            pl.when(place(kind) < 3 - d)(functools.partial(drain, sem, yr.at[kind, d]))
    drain(9, cr.at[both])
    drain(10, xs.at[both])
    drain(11, ps.at[both])
    drain(18, gv.at[:, pl.ds(0, tokens)])
    drain(19, s1)
    drain(20, s2)
    drain(21, sx)
    drain(22, rz)
    drain(23, rz)


def mixed_delta(x, q, k, t, w, a, attn_scale, loss_scale):
    tokens, half = x.shape
    width = q.shape[1]
    heads = width // HEAD_DIM
    rows_dev = a.shape[0]
    groups = GROUPS
    per_group = heads // groups
    mine = per_group // 2
    cols = per_group * HEAD_DIM
    two = 2 * rows_dev
    piece = tokens // 2 // CHUNKS
    state = (HEAD_DIM, HEAD_DIM)
    vmem = pltpu.VMEM
    dma = pltpu.SemaphoreType.DMA
    scratch = [
        vmem((2, tokens, half), BF16),
        vmem((8, tokens, HEAD_DIM), BF16),
        vmem((8 * HEAD_DIM, 2 * tokens), BF16),
        vmem((2, CHUNKS, piece, half), BF16),
        vmem((tokens, width), BF16),
        vmem((tokens, width), BF16),
        vmem((tokens, width), BF16),
        vmem((3, half, width), BF16),
        vmem((rows_dev, width), F32),
        vmem((heads, HEAD_DIM, tokens), BF16),
        vmem((heads, HEAD_DIM, tokens), BF16),
        vmem((heads, tokens, tokens), BF16),
        vmem((heads, tokens, tokens), BF16),
        vmem((heads, tokens, 2 * HEAD_DIM), BF16),
        vmem((tokens, width), F32),
        vmem((tokens, width), BF16),
        vmem((tokens, width), BF16),
        vmem((tokens, width), F32),
        vmem((3, groups, 2, mine, *state), BF16),
        vmem((3, groups, mine, *state), BF16),
        vmem((3, groups, mine, *state), BF16),
        vmem((3, 3, groups, mine, *state), BF16),
        vmem((3, groups, mine, *state), BF16),
        vmem((3, groups, mine, *state), BF16),
        vmem((3, groups, mine, *state), BF16),
        vmem((3, groups, 2, mine, *state), BF16),
        vmem((groups, 2 * tokens, cols), BF16),
        vmem((groups, 2, two, cols // 2), F32),
        vmem((groups, 2, two, cols // 2), BF16),
        vmem((groups, 2, two, cols // 2), BF16),
        vmem((groups, 2, two, cols), BF16),
        vmem((groups, 2, two, cols), BF16),
        vmem((groups, two, cols), F32),
        vmem((groups, rows_dev, cols), BF16),
        vmem((groups, rows_dev, cols), BF16),
        vmem((groups, rows_dev, cols), BF16),
        vmem((groups, 3, rows_dev // 4, cols), BF16),
        vmem((groups, rows_dev // 4, cols), BF16),
        vmem((rows_dev, width), BF16),
        vmem((heads, *state), F32),
        dma((8,)),
        dma((24,)),
        dma((4, CHUNKS)),
        dma((2, 4)),
        dma((5,)),
        dma((3,)),
        dma((groups,)),
        dma((2, groups, 3)),
        dma((groups,)),
        dma((groups,)),
        dma((groups,)),
        dma((groups, 2)),
        dma((groups, 2)),
        dma((groups,)),
        dma((groups, 3)),
        dma((groups, 3)),
        pltpu.SemaphoreType.REGULAR,
        pltpu.SemaphoreType.REGULAR,
        pltpu.SemaphoreType.REGULAR,
    ]
    return pl.pallas_call(
        functools.partial(kernel, attn_scale, loss_scale),
        out_shape=jax.ShapeDtypeStruct((rows_dev, width), BF16),
        in_specs=[pl.BlockSpec(memory_space=pl.ANY)] * 6,
        out_specs=pl.BlockSpec(memory_space=pltpu.VMEM),
        scratch_shapes=scratch,
        compiler_params=pltpu.CompilerParams(
            collective_id=0, has_side_effects=True, vmem_limit_bytes=60 * 1024 * 1024
        ),
    )(x, q, k, t, w, a)


def local(inputs, queries, keys, targets, value_weight, anchor, momentum):
    sequence = queries.shape[1] * lax.axis_size("ctx")
    attn_scale = 1.0 / math.sqrt(HEAD_DIM * sequence)
    loss_scale = 1.0 / math.sqrt(sequence)
    mixed = mixed_delta(
        inputs[0], queries[0], keys[0], targets[0], value_weight[0], anchor, attn_scale, loss_scale
    )
    momentum_next = slow_decay * momentum + mixed.astype(F32)
    anchor_next = anchor - outer_rate * inner_rate * momentum_next
    return (anchor_next[None], momentum_next[None])


def solution(mesh):
    placed = (
        P("rep", "ctx", "head"),
        P("rep", "ctx", "head"),
        P("rep", "ctx", "head"),
        P("rep", "ctx", "head"),
        P("rep", None, "head"),
        P("ctx", "head"),
        P("ctx", "head"),
    )
    return jax.shard_map(
        local,
        mesh=mesh,
        in_specs=placed,
        out_specs=(P("rep", "ctx", "head"), P("rep", "ctx", "head")),
        check_vma=False,
    )
```

time: 93.8 us -> 88.1 us (0.939); the launches traced: 93.7 us -> 86.9 us
  Pallas kernels: 90.9 us -> 84.2 us
    pallas_call x1, Pallas kernels: 90.9 us -> 84.2 us  [mixed_delta(): pl.pallas_call(functools.partial(kernel, attn_scale, loss_scale), out_sha...]
where the time goes in v2:
time: 88.1 us; the launch traced here: 86.9 us
  Pallas kernels  84.2 us (96%)
  other arithmetic  2.09 us (2%)
    pallas_call x1, Pallas kernels, mixed_delta(): pl.pallas_call(functools.partial(kernel, attn_scale, loss_scale), out_sha...  84.2 us
    broadcast_in_dim x1, other arithmetic, local(): return (anchor_next[None], momentum_next[None])  2.09 us

profile of v2, /device:TPU:4, one launch (start us, length us, event | category | flops | bytes accessed | tf_op | source)
XLA Modules:
  0.0 86.9 jit_solution(5157605933338769342)
XLA Ops:
  0.6 0.0 copy-start
  0.6 0.0 copy-start.1
  0.7 84.2 %shard_map.86 = bf16[128,1024]{1,0:T(8,128)(2,1)} custom-call(bf16[512,1024]{1,0:T(8,128)(2,1)} %bitcast.10, bf16[512,1024]{1,0:T(8,128)(2,1)} %bitcast.11, bf16[512,1024]{1,0:T(8,128)(2,1)} %bitcast.12, bf16[512,1024]{1,0:T(8,128)(2,1)} %bitcast.13, bf16[2048,1024]{1,0:T(8,128)(2,1)} %bitcast.9, f32[128,1024]{1,0:T(8,128)} %a_ref.1), custom_call_target="tpu_custom_call" | custom-call | tf_op jit(solution)/shard_map/pallas_call | solution.py:734
  84.8 0.0 copy-done
  84.8 0.0 copy-done.1
  84.8 2.1 %fusion = (f32[1,128,1024]{2,1,0:T(8,128)}, f32[1,128,1024]{2,1,0:T(8,128)}) fusion(bf16[128,1024]{1,0:T(8,128)(2,1)} %shard_map.86, f32[128,1024]{1,0:T(8,128)S(1)} %copy-done.1, f32[128,1024]{1,0:T(8,128)S(1)} %copy-done), kind=kLoop, calls=%fused_computation.2 | loop fusion | flops 655360 | bytes 2359296 | tf_op jit(solution)/shard_map/broadcast_in_dim | solution.py:755
Async XLA Ops:
  0.6 84.2 %copy-start = (f32[128,1024]{1,0:T(8,128)S(1)}, f32[128,1024]{1,0:T(8,128)}, u32[]{:S(2)}) copy-start(f32[128,1024]{1,0:T(8,128)} %a_ref.1) | copy-start | bytes 1572868
  0.6 84.2 %copy-start.1 = (f32[128,1024]{1,0:T(8,128)S(1)}, f32[128,1024]{1,0:T(8,128)}, u32[]{:S(2)}) copy-start(f32[128,1024]{1,0:T(8,128)} %param.13) | copy-start | bytes 1572868

commit v3 on v2

--- a/solution.py
+++ b/solution.py
@@ -10,17 +10,19 @@
 
 HEAD_DIM = 128
 GROUPS = 4
+WIDE = 1
 CHUNKS = 4
 MESH = pl.DeviceIdType.MESH
 
 ORDER = (
-    ("state", 0), ("later", 0), ("state", 1), ("a_rest", 0), ("y", 0), ("state", 2), ("later", 1), ("state", 3),
-    ("later", 2), ("y", 1), ("later", 3), ("x", 0), ("base", 0), ("y", 2), ("base", 1), ("y", 3), ("x", 1),
-    ("back", 0), ("prepare", 0), ("x", 2), ("know", 0), ("grad", 0), ("x", 3), ("back", 1), ("r1", 0), ("base", 2), ("sides", 0),
-    ("grad", 1), ("back", 2), ("r1", 1), ("r2", 0), ("back", 3), ("base", 3), ("grad", 2), ("own", 0), ("sides", 1), ("r1", 2),
-    ("r2", 1), ("grad", 3), ("rx", 0), ("r1", 3), ("sides", 2), ("r2", 2), ("own", 1), ("sides", 3), ("know_all", 0), ("rz", 0), ("r2", 3),
-    ("rx", 1), ("own", 2), ("rz", 1), ("own", 3), ("rx", 2), ("mix", 0), ("rz", 2), ("mix", 1), ("rx", 3), ("rz", 3), ("end", 0), ("mix", 2), ("end", 1),
-    ("mix", 3), ("end", 2), ("end", 3),
+    ("state", 0), ("later", 0), ("a_rest", 0), ("state", 1), ("prepare", 0), ("y", 0), ("state", 3), ("later", 1),
+    ("later", 3), ("state", 2), ("base", 1), ("y", 1), ("base", 3), ("base", 2), ("base", 0), ("x", 0),
+    ("know", 0), ("y", 3), ("later", 2), ("y", 2), ("x", 1), ("back", 0), ("grad", 0), ("x", 3),
+    ("back", 1), ("x", 2), ("r1", 0), ("grad", 1), ("back", 3), ("own", 0), ("sides", 0), ("back", 2),
+    ("w0", 1), ("r2", 0), ("grad", 3), ("wo", 1), ("grad", 2), ("r1", 3), ("own", 3), ("sides", 3),
+    ("r1", 2), ("rx", 0), ("own", 2), ("sides", 2), ("r2", 3), ("w1", 1), ("r2", 2), ("rz", 0),
+    ("rx", 3), ("w2", 1), ("mix", 0), ("rz", 3), ("rx", 2), ("rz", 1), ("end", 0), ("rz", 2),
+    ("mix", 3), ("mix", 1), ("mix", 2), ("end", 3), ("end", 1), ("end", 2),
 )
 
 inner_rate = 0.05
@@ -59,13 +61,14 @@
     wv,
     av,
     qt,
-    kt,
+    kq,
     sc,
     sct,
     wqk,
     vp,
     vv,
-    gl,
+    ww,
+    qtt,
     base,
     st,
     cr,
@@ -89,9 +92,14 @@
     mz,
     mixb,
     uu,
+    wx,
+    wo,
+    w1,
+    w2,
     load_sem,
     sent,
     f_recv,
+    h_recv,
     p_recv,
     a_recv,
     ay_recv,
@@ -105,6 +113,7 @@
     rx_recv,
     rz_recv,
     mz_recv,
+    w_recv,
     y_known,
     low_known,
     high_known,
@@ -135,13 +144,17 @@
     y_far = (lax.rem(y + 2, 4) * 4 + low, rep, head)
     z_up = (me, lax.rem(rep + 1, 8), head)
     z_down = (me, lax.rem(rep + 7, 8), head)
-    z_ids = [lax.rem(zk + d, 4) for d in (1, 2, 3)]
-    z_peers = [(me, rep - zk + z, head) for z in z_ids]
+    inner = (zk > 0) & (zk < 3)
+    z_peers = [(me, rep - zk + lax.rem(zk + d, 4), head) for d in (1, 2, 3)]
+    owners = [(me, rep - zk + z, head) for z in (1, 2)]
 
     def remote(src, dst, send, recv, peer):
         return pltpu.make_async_remote_copy(
             src_ref=src, dst_ref=dst, send_sem=send, recv_sem=recv, device_id=peer, device_id_type=MESH
         )
+
+    def arrived(sem, ref):
+        pltpu.make_async_copy(ref, ref, sem).wait()
 
     own_rows = pl.ds(pl.multiple_of(head * half, half), half)
     other_rows = pl.ds(pl.multiple_of((1 - head) * half, half), half)
@@ -184,36 +197,22 @@
                 remote(x_ref.at[pl.ds(at, piece)], rel.at[side, n], sent.at[0], f_recv.at[side, n], peer)
             )
             first[-1].start()
-    swaps = []
     for n in range(4):
         src = x_ref.at[:, lanes(2 * n + 1 - core)]
-        swaps.append(remote(src, xp.at[head * 4 + n], sent.at[2], p_recv.at[0, n], core_peer))
-        swaps[-1].start()
+        remote(src, xp.at[head * 4 + n], sent.at[0], p_recv.at[0], core_peer).start()
 
     tell(y_known, y_down)
-    inner = (zk > 0) & (zk < 3)
 
     @pl.when(inner)
     def _():
         tell(low_known, z_down)
         tell(high_known, z_up)
 
-    second = []
-
     def relay(n):
         for side, peer in ((0, far_peer), (1, x_peer)):
             first[2 * n + side].wait_recv()
             at = side * (tokens // 2) + n * piece
-            second.append(
-                remote(
-                    rel.at[side, n],
-                    x2.at[1, pl.ds(at, piece)],
-                    sent.at[1],
-                    f_recv.at[2 + side, n],
-                    peer,
-                )
-            )
-            second[-1].start()
+            remote(rel.at[side, n], x2.at[1, pl.ds(at, piece)], sent.at[0], h_recv.at[n // 2], peer).start()
 
     loads[0].wait()
     loads[1].wait()
@@ -226,7 +225,7 @@
         q_t = q.T
         k_t = k.T
         qt[h] = q_t
-        kt[h] = k_t
+        kq[h, :HEAD_DIM] = k_t
         row = lax.broadcasted_iota(jnp.int32, (mid, mid), 0)
         col = lax.broadcasted_iota(jnp.int32, (mid, mid), 1)
         lower = row >= col
@@ -237,12 +236,28 @@
             sct[h, rows, rows] = jnp.where(upper, dot(k[rows], q_t[:, rows]), 0.0).astype(BF16)
         sc[h, mid:, :mid] = dot(q[mid:], k_t[:, :mid]).astype(BF16)
         sct[h, :mid, mid:] = dot(k[:mid], q_t[:, mid:]).astype(BF16)
-        wqk[h, :mid, :HEAD_DIM] = (gc * dot(sct[h, :mid, :], q)).astype(BF16)
-        wqk[h, mid:, :HEAD_DIM] = (gc * dot(sct[h, mid:, mid:], q[mid:])).astype(BF16)
         wqk[h, :, HEAD_DIM:] = k
         st[0, h // per_group, lax.rem(h, per_group) // mine, lax.rem(h, mine)] = dot(q_t, q).astype(BF16)
         return carry
 
+    def products(h, carry):
+        at = lanes(h)
+        q = qv[:, at]
+        t = tv[:, at]
+        q_t = qt[h]
+        wqk[h, :mid, :HEAD_DIM] = (gc * dot(sct[h, :mid, :], q)).astype(BF16)
+        wqk[h, mid:, :HEAD_DIM] = (gc * dot(sct[h, mid:, mid:], q[mid:])).astype(BF16)
+        kq[h, HEAD_DIM:, :mid] = (gc * dot(q_t, sc[h, :, :mid])).astype(BF16)
+        kq[h, HEAD_DIM:, mid:] = (gc * dot(q_t[:, mid:], sc[h, mid:, mid:])).astype(BF16)
+        qtt[h] = -loss_scale * dot(q_t, t)
+        base[:mid, at] = -loss_scale * dot(sct[h, :mid, :], t)
+        base[mid:, at] = -loss_scale * dot(sct[h, mid:, mid:], t[mid:])
+        low = dot(sct[h, :mid, mid:], sc[h, mid:, :])
+        ww[h, :mid, :mid] = (gc * (low[:, :mid] + dot(sct[h, :mid, :mid], sc[h, :mid, :mid]))).astype(BF16)
+        ww[h, :mid, mid:] = (gc * low[:, mid:]).astype(BF16)
+        ww[h, mid:, :] = (gc * dot(sct[h, mid:, mid:], sc[h, mid:, :])).astype(BF16)
+        return carry
+
     lax.fori_loop(0, heads, scores, 0)
 
     both = pl.ds(1, 2)
@@ -254,22 +269,22 @@
     def core_copy(kinds, g, sem, recv):
         return remote(st.at[kinds, g, 1 - core], cr.at[kinds, g], sent.at[sem], recv, core_peer)
 
-    def y_copies(kind, g, recv, sem):
+    def y_copies(kind, g, recv):
         ahead, behind = (y_up, y_down) if kind == 1 else (y_down, y_up)
         return [
-            remote(tt.at[kind, g], yr.at[kind, d, g], sent.at[sem + d], recv.at[d], peer)
+            remote(tt.at[kind, g], yr.at[kind, d, g], sent.at[3], recv, peer)
             for d, peer in enumerate((ahead, y_far, behind))
         ]
 
-    def y_send(kind, g, recv, sem):
+    def y_send(kind, g, recv):
         total = st[kind, g, core].astype(F32) + cr[kind, g].astype(F32)
         tt[kind, g] = total.astype(BF16)
-        for d, copy in enumerate(y_copies(kind, g, recv, sem)):
+        for d, copy in enumerate(y_copies(kind, g, recv)):
             pl.when(place(kind) < 3 - d)(copy.start)
 
-    def y_wait(kind, g, recv, sem):
-        for d, copy in enumerate(y_copies(kind, g, recv, sem)):
-            pl.when(place(kind) > d)(copy.wait_recv)
+    def y_wait(kind, g, recv):
+        for d in (1, 2, 3):
+            pl.when(place(kind) == d)(functools.partial(arrived, recv, yr.at[kind, pl.ds(0, d), g]))
 
     def earlier(kind, g):
         return yr[kind, 0, g].astype(F32) + yr[kind, 1, g].astype(F32) + yr[kind, 2, g].astype(F32)
@@ -295,13 +310,16 @@
     every = pl.ds(0, GROUPS)
     head_start = pl.ds(0, 1)
     rest = pl.ds(1, GROUPS - 1)
-    a_core = core_copy(alone, every, 3, a_recv.at[0])
-    a_x = [x_copy(alone, part, 4, a_recv.at[1 + n]) for n, part in enumerate((head_start, rest))]
-    a_back = [back_copy(alone, part, 5, a_recv.at[3 + n]) for n, part in enumerate((head_start, rest))]
-    ay = (0, every, ay_recv, 6)
+    a_core = core_copy(alone, every, 2, a_recv.at[0])
+    a_x = [x_copy(alone, part, 2, a_recv.at[1 + n]) for n, part in enumerate((head_start, rest))]
+    a_back = [back_copy(alone, part, 2, a_recv.at[3 + n]) for n, part in enumerate((head_start, rest))]
+    ay = (0, every, ay_recv.at[0])
     a_core.start()
 
     relay(0)
+    a_core.wait_recv()
+    pl.semaphore_wait(y_known, 1)
+    y_send(*ay)
     relay(1)
 
     loads[2].wait()
@@ -315,76 +333,67 @@
 
     lax.fori_loop(0, width // wide, partial, 0)
 
-    a_core.wait_recv()
-    pl.semaphore_wait(y_known, 1)
-    y_send(*ay)
+    loads[4].wait()
+    lax.fori_loop(0, 2, products, 0)
     relay(2)
+    lax.fori_loop(2, 4, products, 0)
     relay(3)
+    y_wait(*ay)
+    for copy, which in zip(a_x, (head_start, rest)):
+        x_fill(0, which)
+        copy.start()
+    lax.fori_loop(4, heads, products, 0)
 
     def turn_own(side):
         def turn(n, carry):
-            at = lanes(((head + side) % 2) * 4 + n)
-            xt[at, :tokens] = x2[side, :, lanes(2 * n + core)].T
+            block = lax.rem(head + side, 2) * 4 + n
+            xt[block // 2, lax.rem(block, 2), :, :tokens] = x2[side, :, lanes(2 * n + core)].T
             return carry
 
         lax.fori_loop(0, 4, turn, 0)
 
     def turn_theirs(side):
         def turn(n, carry):
-            block = ((head + side) % 2) * 4 + n
-            xt[lanes(block), tokens:] = xp[block].T
+            block = lax.rem(head + side, 2) * 4 + n
+            xt[block // 2, lax.rem(block, 2), :, tokens:] = xp[block].T
             return carry
 
         lax.fori_loop(0, 4, turn, 0)
 
     turn_own(0)
-    for copy in swaps:
-        copy.wait_recv()
+    arrived(p_recv.at[0], xp.at[pl.ds(0, 4)])
     turn_theirs(0)
-    loads[4].wait()
     loads[5].wait()
-    y_wait(*ay)
-    x_fill(0, head_start)
-    a_x[0].start()
-    x_fill(0, rest)
 
     def finish(n):
-        for side in range(2):
-            for m in (2 * n, 2 * n + 1):
-                second[2 * m + side].wait_recv()
-        if n == 1:
-            a_x[1].start()
         size = 2 * piece
+        arrived(h_recv.at[n], x2.at[1, pl.ds(0, mid)])
+        parts = [slice(side * mid + n * size, side * mid + (n + 1) * size) for side in range(2)]
 
         def values(m, carry):
             at = lanes(m, wide)
-            for side in range(2):
-                rows = slice(side * mid + n * size, side * mid + (n + 1) * size)
-                vv[rows, at] = (vp[rows, at] + dot(x2[1, rows, :], wv[1, :, at])).astype(BF16)
+            rows = jnp.concatenate([x2[1, p, :] for p in parts], axis=0)
+            got = dot(rows, wv[1, :, at])
+            for i, p in enumerate(parts):
+                vv[p, at] = (vp[p, at] + got[i * size : (i + 1) * size]).astype(BF16)
             return carry
 
         lax.fori_loop(0, width // wide, values, 0)
 
     finish(0)
+    a_x[0].wait_recv()
+    back_fill(0, head_start)
+    a_back[0].start()
     finish(1)
     for n in range(4):
         src = x2.at[1, :, lanes(2 * n + 1 - core)]
-        swaps.append(remote(src, xp.at[(1 - head) * 4 + n], sent.at[2], p_recv.at[1, n], core_peer))
-        swaps[-1].start()
-    a_x[0].wait_recv()
-    back_fill(0, head_start)
-    a_back[0].start()
-
+        remote(src, xp.at[(1 - head) * 4 + n], sent.at[0], p_recv.at[1], core_peer).start()
     def states(h, carry):
         at = lanes(h)
         g, which, n = h // per_group, lax.rem(h, per_group) // mine, lax.rem(h, mine)
-        v = vv[:, at]
-        st[1, g, which, n] = dot(kt[h], v).astype(BF16)
-        top = dot(sc[h, :mid, :mid], v[:mid])
-        bottom = dot(sc[h, mid:, :], v)
-        gl[:mid, at] = (gc * top - loss_scale * tv[:mid, at].astype(F32)).astype(BF16)
-        gl[mid:, at] = (gc * bottom - loss_scale * tv[mid:, at].astype(F32)).astype(BF16)
-        uu[h] = dot(qt[h], gl[:, at])
+        both_states = dot(kq[h], vv[:, at])
+        st[1, g, which, n] = both_states[:HEAD_DIM].astype(BF16)
+        uu[h] = both_states[HEAD_DIM:] + qtt[h]
         return carry
 
     def with_later(h, carry):
@@ -394,8 +403,7 @@
 
     def bases(h, carry):
         at = lanes(h)
-        base[:mid, at] = dot(sct[h, :mid, :], gl[:, at])
-        base[mid:, at] = dot(sct[h, mid:, mid:], gl[mid:, at])
+        base[:, at] += dot(ww[h], vv[:, at])
         return carry
 
     def over(body, g):
@@ -403,7 +411,7 @@
 
     def gv_copy(g):
         return remote(
-            gv.at[g, pl.ds(0, tokens)], gv.at[g, pl.ds(tokens, tokens)], sent.at[18], g_recv.at[g], core_peer
+            gv.at[g, pl.ds(0, tokens)], gv.at[g, pl.ds(tokens, tokens)], sent.at[1], g_recv.at[g], core_peer
         )
 
     def grads(g):
@@ -426,18 +434,21 @@
     part = cols // 2
 
     def block(g, to):
-        return dot(xt[pl.ds(pl.multiple_of(to * two, two), two), :], gv[g])
+        return dot(xt[to].reshape(two, 2 * tokens), gv[g])
+
+    def strip(g, to):
+        return dot(xt[:, to].reshape(4 * rows_dev, 2 * tokens), gv[g]).reshape(4, rows_dev, cols)
 
     def r1_copies(g):
         return (
-            remote(s1.at[g, 0], r1.at[g, 0], sent.at[19], r1_recv.at[g, 0], y_up),
-            remote(s1.at[g, 1], r1.at[g, 1], sent.at[19], r1_recv.at[g, 1], y_down),
+            remote(s1.at[g, 0], r1.at[g, 0], sent.at[2], r1_recv.at[g], y_up),
+            remote(s1.at[g, 1], r1.at[g, 1], sent.at[2], r1_recv.at[g], y_down),
         )
 
     def r2_copies(g):
         return (
-            remote(s2.at[g, 0], r2.at[g, 0], sent.at[20], r2_recv.at[g, 0], y_up),
-            remote(s2.at[g, 1], r2.at[g, 1], sent.at[20], r2_recv.at[g, 1], y_down),
+            remote(s2.at[g, 0], r2.at[g, 0], sent.at[2], r2_recv.at[g], y_up),
+            remote(s2.at[g, 1], r2.at[g, 1], sent.at[2], r2_recv.at[g], y_down),
         )
 
     def reduce_one(g):
@@ -457,10 +468,8 @@
         keep[g, 1] = down[:, part:]
 
     def reduce_two(g):
-        one = r1_copies(g)
-        one[0].wait_recv()
+        arrived(r1_recv.at[g], r1.at[g])
         s2[g, 0, :, :part] = (keep[g, 0] + r1[g, 0].astype(F32)).astype(BF16)
-        one[1].wait_recv()
         s2[g, 1, :, part:] = (keep[g, 1] + r1[g, 1].astype(F32)).astype(BF16)
         for copy in r2_copies(g):
             copy.start()
@@ -469,78 +478,119 @@
         own[g] = block(g, y)
 
     def rx_copy(g):
-        return remote(sx.at[g], rx.at[g], sent.at[21], rx_recv.at[g], x_peer)
+        return remote(sx.at[g], rx.at[g], sent.at[2], rx_recv.at[g], x_peer)
 
     def block_rows(which):
         return pl.ds(pl.multiple_of(which * rows_dev, rows_dev), rows_dev)
 
     def reduce_x(g):
-        for copy in r2_copies(g):
-            copy.wait_recv()
+        arrived(r2_recv.at[g], r2.at[g])
         rows = block_rows(1 - xl)
         sx[g] = (own[g, rows, :] + r2[g, 0, rows, :].astype(F32) + r2[g, 1, rows, :].astype(F32)).astype(BF16)
         copy = rx_copy(g)
         copy.start()
 
-    share = rows_dev // 4
-
-    def piece_rows(which):
-        return pl.ds(pl.multiple_of(which * share, share), share)
+    def wx_copy():
+        return remote(wx.at[0], wx.at[1], sent.at[1], w_recv.at[0], x_peer)
+
+    def wide_out(g):
+        arrived(g_recv.at[g], gv.at[g, pl.ds(0, tokens)])
+        wx[0] = strip(g, 1 - xl).astype(BF16)
+        wx_copy().start()
+
+    def wide_own(g):
+        wo[...] = strip(g, xl)
+
+    def wide_block(at):
+        return wo[at] + wx[1, at].astype(F32)
+
+    def w1_copies():
+        return [remote(w1.at[0, n], w1.at[1, n], sent.at[2], w_recv.at[1], p) for n, p in enumerate((y_up, y_down))]
+
+    def w2_copies():
+        return [remote(w2.at[0, n], w2.at[1, n], sent.at[2], w_recv.at[2], p) for n, p in enumerate((y_up, y_down))]
+
+    def wide_one(g):
+        wx_copy().wait_recv()
+        across = wide_block(lax.rem(y + 2, 4)).astype(BF16)
+        w1[0, 0] = across[:, :part]
+        w1[0, 1] = across[:, part:]
+        for copy in w1_copies():
+            copy.start()
+
+    def wide_two(g):
+        up = wide_block(lax.rem(y + 1, 4))
+        down = wide_block(lax.rem(y + 3, 4))
+        arrived(w_recv.at[1], w1.at[1])
+        w2[0, 0, :, :part] = (up[:, :part] + w1[1, 0].astype(F32)).astype(BF16)
+        w2[0, 0, :, part:] = up[:, part:].astype(BF16)
+        w2[0, 1, :, :part] = down[:, :part].astype(BF16)
+        w2[0, 1, :, part:] = (down[:, part:] + w1[1, 1].astype(F32)).astype(BF16)
+        for copy in w2_copies():
+            copy.start()
+
+    share = rows_dev // 2
+    own_share = pl.ds(pl.multiple_of(jnp.where(zk == 2, share, 0), share), share)
 
     def rz_copies(g):
         return [
-            remote(dz.at[g, piece_rows(z)], rz.at[g, n], sent.at[22], rz_recv.at[g, n], peer)
-            for n, (z, peer) in enumerate(zip(z_ids, z_peers))
+            remote(
+                dz.at[g, pl.ds(n * share, share)],
+                rz.at[g, zk - jnp.where(zk > n + 1, 1, 0)],
+                sent.at[4],
+                rz_recv.at[g],
+                owners[n],
+            )
+            for n in range(2)
         ]
 
     def reduce_z(g):
-        rx_copy(g).wait_recv()
-        rows = block_rows(xl)
         at = slice(g * cols, (g + 1) * cols)
-        total = own[g, rows, :] + r2[g, 0, rows, :].astype(F32) + r2[g, 1, rows, :].astype(F32)
+        if g == WIDE:
+            arrived(w_recv.at[2], w2.at[1])
+            total = wide_block(y) + w2[1, 0].astype(F32) + w2[1, 1].astype(F32)
+        else:
+            rx_copy(g).wait_recv()
+            rows = block_rows(xl)
+            total = own[g, rows, :] + r2[g, 0, rows, :].astype(F32) + r2[g, 1, rows, :].astype(F32)
+            total += rx[g].astype(F32)
         drift = (av[:, at] - wv[2, :rows_dev, at].astype(F32)) / inner_rate
-        dz[g] = (total + rx[g].astype(F32) + drift).astype(BF16)
-        for copy in rz_copies(g):
-            copy.start()
-
-    def mz_copies(g):
-        at = slice(g * cols, (g + 1) * cols)
-        return [
-            remote(mz.at[g], mixb.at[piece_rows(zk), at], sent.at[23], mz_recv.at[g, n], peer)
-            for n, peer in enumerate(z_peers)
-        ]
+        dz[g] = (total + drift).astype(BF16)
+        for n, copy in enumerate(rz_copies(g)):
+            pl.when(zk != n + 1)(copy.start)
 
     def mix(g):
-        for copy in rz_copies(g):
-            copy.wait_recv()
-        at = slice(g * cols, (g + 1) * cols)
-        total = dz[g, piece_rows(zk), :].astype(F32)
-        for n in range(3):
-            total += rz[g, n].astype(F32)
-        mean = (0.25 * total).astype(BF16)
-        mz[g] = mean
-        mixb[piece_rows(zk), at] = mean
-        for copy in mz_copies(g):
-            copy.start()
+        @pl.when(inner)
+        def _():
+            arrived(rz_recv.at[g], rz.at[g])
+            at = slice(g * cols, (g + 1) * cols)
+            total = dz[g, own_share, :].astype(F32)
+            for n in range(3):
+                total += rz[g, n].astype(F32)
+            mean = (0.25 * total).astype(BF16)
+            mz[g] = mean
+            mixb[own_share, at] = mean
+            for peer in z_peers:
+                remote(mz.at[g], mixb.at[own_share, at], sent.at[4], mz_recv.at[g], peer).start()
 
     def settle(g):
-        for copy in mz_copies(g):
-            copy.wait_recv()
+        pl.when(inner)(functools.partial(arrived, mz_recv.at[g], mz.at[g]))
+        pl.when(~inner)(functools.partial(arrived, mz_recv.at[g], dz.at[g]))
 
     loads[6].wait()
     loads[7].wait()
 
     def scan_core(g):
-        return core_copy(both, pl.ds(g, 1), 9, c_recv.at[g])
+        return core_copy(both, pl.ds(g, 1), 1, c_recv.at[g])
 
     def scan_x(g):
-        return x_copy(both, pl.ds(g, 1), 10, x_recv.at[g])
+        return x_copy(both, pl.ds(g, 1), 1, x_recv.at[g])
 
     def scan_back(g):
-        return back_copy(both, pl.ds(g, 1), 11, b_recv.at[g])
+        return back_copy(both, pl.ds(g, 1), 1, b_recv.at[g])
 
     def y_args(kind, g):
-        return (kind, pl.ds(g, 1), y_recv.at[kind - 1, g], 12 + 3 * (kind - 1))
+        return (kind, pl.ds(g, 1), y_recv.at[kind - 1, g])
 
     def state_step(g):
         over(states, g)
@@ -582,29 +632,17 @@
 
     def prepare(g):
         turn_own(1)
-        for copy in swaps[4:]:
-            copy.wait_recv()
+        arrived(p_recv.at[1], xp.at[pl.ds(0, 4)])
         turn_theirs(1)
 
     def know(g):
-        @pl.when(zk == 1)
+        @pl.when(zk < 2)
         def _():
             pl.semaphore_wait(low_known, 1)
-            tell(low_known, z_down)
-
-        @pl.when(zk == 2)
+
+        @pl.when(zk >= 2)
         def _():
             pl.semaphore_wait(high_known, 1)
-            tell(high_known, z_up)
-
-    def know_all(g):
-        @pl.when(zk == 0)
-        def _():
-            pl.semaphore_wait(low_known, 2)
-
-        @pl.when(zk == 3)
-        def _():
-            pl.semaphore_wait(high_known, 2)
 
     steps = {
         "state": state_step,
@@ -616,8 +654,11 @@
         "base": base_step,
         "prepare": prepare,
         "know": know,
-        "know_all": know_all,
         "grad": grad_step,
+        "w0": wide_out,
+        "wo": wide_own,
+        "w1": wide_one,
+        "w2": wide_two,
         "r1": reduce_one,
         "sides": sides,
         "r2": reduce_two,
@@ -635,25 +676,14 @@
     def drain(sem, ref):
         remote(ref, ref, sent.at[sem], sent.at[sem], core_peer).wait_send()
 
-    drain(0, rel)
-    drain(1, x2.at[1])
-    drain(2, xp)
-    drain(3, cr.at[alone])
-    drain(4, xs.at[alone])
-    drain(5, ps.at[alone])
-    for kind in range(3):
-        for d in range(3):
-            sem = 6 + d if kind == 0 else 12 + 3 * (kind - 1) + d
-            pl.when(place(kind) < 3 - d)(functools.partial(drain, sem, yr.at[kind, d]))
-    drain(9, cr.at[both])
-    drain(10, xs.at[both])
-    drain(11, ps.at[both])
-    drain(18, gv.at[:, pl.ds(0, tokens)])
-    drain(19, s1)
-    drain(20, s2)
-    drain(21, sx)
-    drain(22, rz)
-    drain(23, rz)
+    drain(0, wv.at[pl.ds(0, 3), pl.ds(0, tokens)])
+    drain(1, x2)
+    drain(2, vp.at[pl.ds(0, 15 * tokens // 16)])
+    unit = tokens // 8
+    for n in range(4):
+        pl.when(y == n)(functools.partial(drain, 3, vv.at[pl.ds(0, (3 + n) * unit)]))
+    pl.when(inner)(functools.partial(drain, 4, vv.at[pl.ds(0, tokens // 2)]))
+    pl.when(~inner)(functools.partial(drain, 4, dz))
 
 
 def mixed_delta(x, q, k, t, w, a, attn_scale, loss_scale):
@@ -673,7 +703,7 @@
     scratch = [
         vmem((2, tokens, half), BF16),
         vmem((8, tokens, HEAD_DIM), BF16),
-        vmem((8 * HEAD_DIM, 2 * tokens), BF16),
+        vmem((4, 2, rows_dev, 2 * tokens), BF16),
         vmem((2, CHUNKS, piece, half), BF16),
         vmem((tokens, width), BF16),
         vmem((tokens, width), BF16),
@@ -681,13 +711,14 @@
         vmem((3, half, width), BF16),
         vmem((rows_dev, width), F32),
         vmem((heads, HEAD_DIM, tokens), BF16),
-        vmem((heads, HEAD_DIM, tokens), BF16),
+        vmem((heads, 2 * HEAD_DIM, tokens), BF16),
         vmem((heads, tokens, tokens), BF16),
         vmem((heads, tokens, tokens), BF16),
         vmem((heads, tokens, 2 * HEAD_DIM), BF16),
         vmem((tokens, width), F32),
         vmem((tokens, width), BF16),
-        vmem((tokens, width), BF16),
+        vmem((heads, tokens, tokens), BF16),
+        vmem((heads, *state), F32),
         vmem((tokens, width), F32),
         vmem((3, groups, 2, mine, *state), BF16),
         vmem((3, groups, mine, *state), BF16),
@@ -707,33 +738,39 @@
         vmem((groups, rows_dev, cols), BF16),
         vmem((groups, rows_dev, cols), BF16),
         vmem((groups, rows_dev, cols), BF16),
-        vmem((groups, 3, rows_dev // 4, cols), BF16),
-        vmem((groups, rows_dev // 4, cols), BF16),
+        vmem((groups, 3, rows_dev // 2, cols), BF16),
+        vmem((groups, rows_dev // 2, cols), BF16),
         vmem((rows_dev, width), BF16),
         vmem((heads, *state), F32),
+        vmem((2, 4, rows_dev, cols), BF16),
+        vmem((4, rows_dev, cols), F32),
+        vmem((2, 2, rows_dev, cols // 2), BF16),
+        vmem((2, 2, rows_dev, cols), BF16),
         dma((8,)),
-        dma((24,)),
-        dma((4, CHUNKS)),
-        dma((2, 4)),
         dma((5,)),
-        dma((3,)),
+        dma((2, CHUNKS)),
+        dma((2,)),
+        dma((2,)),
+        dma((5,)),
+        dma((1,)),
         dma((groups,)),
-        dma((2, groups, 3)),
+        dma((2, groups)),
         dma((groups,)),
         dma((groups,)),
         dma((groups,)),
-        dma((groups, 2)),
-        dma((groups, 2)),
         dma((groups,)),
-        dma((groups, 3)),
-        dma((groups, 3)),
+        dma((groups,)),
+        dma((groups,)),
+        dma((groups,)),
+        dma((groups,)),
+        dma((3,)),
         pltpu.SemaphoreType.REGULAR,
         pltpu.SemaphoreType.REGULAR,
         pltpu.SemaphoreType.REGULAR,
     ]
     return pl.pallas_call(
         functools.partial(kernel, attn_scale, loss_scale),
-        out_shape=jax.ShapeDtypeStruct((rows_dev, width), BF16),
+        out_shape=pltpu.VMEM((rows_dev, width), BF16),
         in_specs=[pl.BlockSpec(memory_space=pl.ANY)] * 6,
         out_specs=pl.BlockSpec(memory_space=pltpu.VMEM),
         scratch_shapes=scratch,

time: 88.1 us -> 81 us (0.919); the launches traced: 86.9 us -> 80.9 us
  Pallas kernels: 84.2 us -> 79.1 us
  other arithmetic: 2.09 us -> 1.14 us
    pallas_call x1, Pallas kernels: 84.2 us -> 79.1 us  [mixed_delta(): pl.pallas_call(functools.partial(kernel, attn_scale, loss_scale), out_sha...]
    broadcast_in_dim x1, other arithmetic: 2.09 us -> 1.14 us  [local(): return (anchor_next[None], momentum_next[None])]
where the time goes in v3:
time: 81 us; the launch traced here: 80.9 us
  Pallas kernels  79.1 us (98%)
  other arithmetic  1.14 us (1%)
    pallas_call x1, Pallas kernels, mixed_delta(): pl.pallas_call(functools.partial(kernel, attn_scale, loss_scale), out_sha...  79.1 us

profile of v3, /device:TPU:4, one launch (start us, length us, event | category | flops | bytes accessed | tf_op | source)
XLA Modules:
  0.0 80.9 jit_solution(11945486751611665441)
XLA Ops:
  0.6 0.0 copy-start
  0.6 0.0 copy-start.1
  0.7 79.1 %shard_map.86 = bf16[128,1024]{1,0:T(8,128)(2,1)S(1)} custom-call(bf16[512,1024]{1,0:T(8,128)(2,1)} %bitcast.10, bf16[512,1024]{1,0:T(8,128)(2,1)} %bitcast.11, bf16[512,1024]{1,0:T(8,128)(2,1)} %bitcast.12, bf16[512,1024]{1,0:T(8,128)(2,1)} %bitcast.13, bf16[2048,1024]{1,0:T(8,128)(2,1)} %bitcast.9, f32[128,1024]{1,0:T(8,128)} %a_ref.1), custom_call_target="tpu_custom_call" | custom-call | tf_op jit(solution)/shard_map/pallas_call | solution.py:771
  79.7 0.0 copy-done
  79.7 0.0 copy-done.1
  79.7 1.1 %fusion = (f32[1,128,1024]{2,1,0:T(8,128)}, f32[1,128,1024]{2,1,0:T(8,128)}) fusion(bf16[128,1024]{1,0:T(8,128)(2,1)S(1)} %shard_map.86, f32[128,1024]{1,0:T(8,128)S(1)} %copy-done.1, f32[128,1024]{1,0:T(8,128)S(1)} %copy-done), kind=kLoop, calls=%fused_computation.2 | loop fusion | flops 655360 | bytes 2359296 | tf_op jit(solution)/shard_map/broadcast_in_dim | solution.py:792
Async XLA Ops:
  0.6 79.1 %copy-start = (f32[128,1024]{1,0:T(8,128)S(1)}, f32[128,1024]{1,0:T(8,128)}, u32[]{:S(2)}) copy-start(f32[128,1024]{1,0:T(8,128)} %a_ref.1) | copy-start | bytes 1572868
  0.6 79.1 %copy-start.1 = (f32[128,1024]{1,0:T(8,128)S(1)}, f32[128,1024]{1,0:T(8,128)}, u32[]{:S(2)}) copy-start(f32[128,1024]{1,0:T(8,128)} %param.13) | copy-start | bytes 1572868

commit v4 on v3

--- a/solution.py
+++ b/solution.py
@@ -10,19 +10,19 @@
 
 HEAD_DIM = 128
 GROUPS = 4
-WIDE = 1
+WIDE = 2
 CHUNKS = 4
 MESH = pl.DeviceIdType.MESH
 
 ORDER = (
-    ("state", 0), ("later", 0), ("a_rest", 0), ("state", 1), ("prepare", 0), ("y", 0), ("state", 3), ("later", 1),
-    ("later", 3), ("state", 2), ("base", 1), ("y", 1), ("base", 3), ("base", 2), ("base", 0), ("x", 0),
-    ("know", 0), ("y", 3), ("later", 2), ("y", 2), ("x", 1), ("back", 0), ("grad", 0), ("x", 3),
-    ("back", 1), ("x", 2), ("r1", 0), ("grad", 1), ("back", 3), ("own", 0), ("sides", 0), ("back", 2),
-    ("w0", 1), ("r2", 0), ("grad", 3), ("wo", 1), ("grad", 2), ("r1", 3), ("own", 3), ("sides", 3),
-    ("r1", 2), ("rx", 0), ("own", 2), ("sides", 2), ("r2", 3), ("w1", 1), ("r2", 2), ("rz", 0),
-    ("rx", 3), ("w2", 1), ("mix", 0), ("rz", 3), ("rx", 2), ("rz", 1), ("end", 0), ("rz", 2),
-    ("mix", 3), ("mix", 1), ("mix", 2), ("end", 3), ("end", 1), ("end", 2),
+    ("state", 0), ("later", 0), ("know", 0), ("a_rest", 0), ("state", 2), ("prepare", 0), ("y", 0), ("later", 2),
+    ("state", 1), ("later", 1), ("state", 3), ("later", 3), ("y", 2), ("base", 0), ("y", 1), ("base", 3),
+    ("y", 3), ("base", 1), ("x", 0), ("base", 2), ("x", 2), ("back", 0), ("x", 1), ("grad", 0),
+    ("back", 2), ("x", 3), ("back", 1), ("r1", 0), ("grad", 2), ("own", 0), ("sides", 0), ("back", 3),
+    ("grad", 1), ("r2", 0), ("w0", 2), ("grad", 3), ("r1", 1), ("own", 1), ("sides", 1), ("wo", 2),
+    ("r1", 3), ("own", 3), ("sides", 3), ("rx", 0), ("r2", 1), ("w1", 2), ("r2", 3), ("rz", 0),
+    ("rx", 1), ("w2", 2), ("mix", 0), ("rx", 3), ("rz", 1), ("rz", 2), ("rz", 3), ("end", 0),
+    ("mix", 1), ("mix", 2), ("mix", 3), ("end", 1), ("end", 2), ("end", 3),
 )
 
 inner_rate = 0.05
@@ -378,12 +378,15 @@
                 vv[p, at] = (vp[p, at] + got[i * size : (i + 1) * size]).astype(BF16)
             return carry
 
-        lax.fori_loop(0, width // wide, values, 0)
+        tiles = width // wide
+        lax.fori_loop(0, tiles // 2, values, 0)
+        if n == 1:
+            a_x[0].wait_recv()
+            back_fill(0, head_start)
+            a_back[0].start()
+        lax.fori_loop(tiles // 2, tiles, values, 0)
 
     finish(0)
-    a_x[0].wait_recv()
-    back_fill(0, head_start)
-    a_back[0].start()
     finish(1)
     for n in range(4):
         src = x2.at[1, :, lanes(2 * n + 1 - core)]
@@ -595,9 +598,13 @@
     def state_step(g):
         over(states, g)
 
+    later_seen = set()
+
     def later_step(g):
-        if g < 2:
-            a_back[g].wait_recv()
+        part = min(g, 1)
+        if part not in later_seen:
+            later_seen.add(part)
+            a_back[part].wait_recv()
         over(with_later, g)
         scan_core(g).start()
 

time: 81 us -> 79.7 us (0.984)
  Pallas kernels: 79.1 us -> 77.7 us
    pallas_call x1, Pallas kernels: 79.1 us -> 77.7 us  [mixed_delta(): pl.pallas_call(functools.partial(kernel, attn_scale, loss_scale), out_sha...]
where the time goes in v4:
time: 79.7 us; the launch traced here: 79.5 us
  Pallas kernels  77.7 us (97%)
  other arithmetic  1.14 us (1%)
    pallas_call x1, Pallas kernels, mixed_delta(): pl.pallas_call(functools.partial(kernel, attn_scale, loss_scale), out_sha...  77.7 us

profile of v4, /device:TPU:4, one launch (start us, length us, event | category | flops | bytes accessed | tf_op | source)
XLA Modules:
  0.0 79.5 jit_solution(9760756192655181612)
XLA Ops:
  0.6 0.0 copy-start
  0.6 0.0 copy-start.1
  0.7 77.7 %shard_map.86 = bf16[128,1024]{1,0:T(8,128)(2,1)S(1)} custom-call(bf16[512,1024]{1,0:T(8,128)(2,1)} %bitcast.10, bf16[512,1024]{1,0:T(8,128)(2,1)} %bitcast.11, bf16[512,1024]{1,0:T(8,128)(2,1)} %bitcast.12, bf16[512,1024]{1,0:T(8,128)(2,1)} %bitcast.13, bf16[2048,1024]{1,0:T(8,128)(2,1)} %bitcast.9, f32[128,1024]{1,0:T(8,128)} %a_ref.1), custom_call_target="tpu_custom_call" | custom-call | tf_op jit(solution)/shard_map/pallas_call | solution.py:778
  78.3 0.0 copy-done
  78.3 0.0 copy-done.1
  78.3 1.1 %fusion = (f32[1,128,1024]{2,1,0:T(8,128)}, f32[1,128,1024]{2,1,0:T(8,128)}) fusion(bf16[128,1024]{1,0:T(8,128)(2,1)S(1)} %shard_map.86, f32[128,1024]{1,0:T(8,128)S(1)} %copy-done.1, f32[128,1024]{1,0:T(8,128)S(1)} %copy-done), kind=kLoop, calls=%fused_computation.2 | loop fusion | flops 655360 | bytes 2359296 | tf_op jit(solution)/shard_map/broadcast_in_dim | solution.py:799
Async XLA Ops:
  0.6 77.7 %copy-start = (f32[128,1024]{1,0:T(8,128)S(1)}, f32[128,1024]{1,0:T(8,128)}, u32[]{:S(2)}) copy-start(f32[128,1024]{1,0:T(8,128)} %a_ref.1) | copy-start | bytes 1572868
  0.6 77.7 %copy-start.1 = (f32[128,1024]{1,0:T(8,128)S(1)}, f32[128,1024]{1,0:T(8,128)}, u32[]{:S(2)}) copy-start(f32[128,1024]{1,0:T(8,128)} %param.13) | copy-start | bytes 1572868

commit v5 on v4

--- a/solution.py
+++ b/solution.py
@@ -110,6 +110,7 @@
     g_recv,
     r1_recv,
     r2_recv,
+    r3_recv,
     rx_recv,
     rz_recv,
     mz_recv,
@@ -442,6 +443,9 @@
     def strip(g, to):
         return dot(xt[:, to].reshape(4 * rows_dev, 2 * tokens), gv[g]).reshape(4, rows_dev, cols)
 
+    def block_rows(which):
+        return pl.ds(pl.multiple_of(which * rows_dev, rows_dev), rows_dev)
+
     def r1_copies(g):
         return (
             remote(s1.at[g, 0], r1.at[g, 0], sent.at[2], r1_recv.at[g], y_up),
@@ -449,10 +453,11 @@
         )
 
     def r2_copies(g):
-        return (
-            remote(s2.at[g, 0], r2.at[g, 0], sent.at[2], r2_recv.at[g], y_up),
-            remote(s2.at[g, 1], r2.at[g, 1], sent.at[2], r2_recv.at[g], y_down),
-        )
+        return [
+            remote(s2.at[g, n, rows], r2.at[g, n, rows], sent.at[2], recv.at[g], peer)
+            for recv, rows in ((r2_recv, block_rows(1 - xl)), (r3_recv, block_rows(xl)))
+            for n, peer in enumerate((y_up, y_down))
+        ]
 
     def reduce_one(g):
         gv_copy(g).wait_recv()
@@ -483,11 +488,8 @@
     def rx_copy(g):
         return remote(sx.at[g], rx.at[g], sent.at[2], rx_recv.at[g], x_peer)
 
-    def block_rows(which):
-        return pl.ds(pl.multiple_of(which * rows_dev, rows_dev), rows_dev)
-
     def reduce_x(g):
-        arrived(r2_recv.at[g], r2.at[g])
+        arrived(r2_recv.at[g], r2.at[g, 0])
         rows = block_rows(1 - xl)
         sx[g] = (own[g, rows, :] + r2[g, 0, rows, :].astype(F32) + r2[g, 1, rows, :].astype(F32)).astype(BF16)
         copy = rx_copy(g)
@@ -553,6 +555,7 @@
             arrived(w_recv.at[2], w2.at[1])
             total = wide_block(y) + w2[1, 0].astype(F32) + w2[1, 1].astype(F32)
         else:
+            arrived(r3_recv.at[g], r2.at[g, 0])
             rx_copy(g).wait_recv()
             rows = block_rows(xl)
             total = own[g, rows, :] + r2[g, 0, rows, :].astype(F32) + r2[g, 1, rows, :].astype(F32)
@@ -770,6 +773,7 @@
         dma((groups,)),
         dma((groups,)),
         dma((groups,)),
+        dma((groups,)),
         dma((3,)),
         pltpu.SemaphoreType.REGULAR,
         pltpu.SemaphoreType.REGULAR,

time: 79.7 us -> 79.1 us (level)
  no operation moved by 1% of the time
where the time goes in v5:
time: 79.1 us; the launch traced here: 78.9 us
  Pallas kernels  77.1 us (97%)
  other arithmetic  1.14 us (1%)
    pallas_call x1, Pallas kernels, mixed_delta(): pl.pallas_call(functools.partial(kernel, attn_scale, loss_scale), out_sha...  77.1 us

profile of v5, /device:TPU:4, one launch (start us, length us, event | category | flops | bytes accessed | tf_op | source)
XLA Modules:
  0.0 78.9 jit_solution(2739187855945663317)
XLA Ops:
  0.6 0.0 copy-start
  0.6 0.0 copy-start.1
  0.7 77.1 %shard_map.86 = bf16[128,1024]{1,0:T(8,128)(2,1)S(1)} custom-call(bf16[512,1024]{1,0:T(8,128)(2,1)} %bitcast.10, bf16[512,1024]{1,0:T(8,128)(2,1)} %bitcast.11, bf16[512,1024]{1,0:T(8,128)(2,1)} %bitcast.12, bf16[512,1024]{1,0:T(8,128)(2,1)} %bitcast.13, bf16[2048,1024]{1,0:T(8,128)(2,1)} %bitcast.9, f32[128,1024]{1,0:T(8,128)} %a_ref.1), custom_call_target="tpu_custom_call" | custom-call | tf_op jit(solution)/shard_map/pallas_call | solution.py:782
  77.7 0.0 copy-done
  77.7 0.0 copy-done.1
  77.8 1.1 %fusion = (f32[1,128,1024]{2,1,0:T(8,128)}, f32[1,128,1024]{2,1,0:T(8,128)}) fusion(bf16[128,1024]{1,0:T(8,128)(2,1)S(1)} %shard_map.86, f32[128,1024]{1,0:T(8,128)S(1)} %copy-done.1, f32[128,1024]{1,0:T(8,128)S(1)} %copy-done), kind=kLoop, calls=%fused_computation.2 | loop fusion | flops 655360 | bytes 2359296 | tf_op jit(solution)/shard_map/broadcast_in_dim | solution.py:803
Async XLA Ops:
  0.6 77.1 %copy-start = (f32[128,1024]{1,0:T(8,128)S(1)}, f32[128,1024]{1,0:T(8,128)}, u32[]{:S(2)}) copy-start(f32[128,1024]{1,0:T(8,128)} %a_ref.1) | copy-start | bytes 1572868
  0.6 77.1 %copy-start.1 = (f32[128,1024]{1,0:T(8,128)S(1)}, f32[128,1024]{1,0:T(8,128)}, u32[]{:S(2)}) copy-start(f32[128,1024]{1,0:T(8,128)} %param.13) | copy-start | bytes 1572868
